TPU v7x, 512 devices: a whole 4x8x8 slice. The times are simulated.
512 devices in a mesh: section: 32 (over y_hi, z, core), dp: 16 (over x, y_lo).
Axes of the slice: x: 4, y: 8 (y_hi: 2, y_lo: 4; y = y_hi * 4 + y_lo), z: 8, core: 2. Of those that a mesh axis runs over, the one named last changes fastest.
Arguments:
- section_inputs: bfloat16 [32, 2048, 4096], P('section', 'dp'), may hold values from -6 to 6
- norm_gain: bfloat16 [32, 4096], P('section'), may hold values from 0.5 to 1.5
- down_proj: bfloat16 [32, 4096, 256], P('section', 'dp'), may hold values from -0.09375 to 0.09375
- up_proj: bfloat16 [32, 256, 4096], P('section', None, 'dp'), may hold values from -0.1875 to 0.1875
- readout_matrix: bfloat16 [4096, 128], P('dp'), may hold values from -0.09375 to 0.09375
- ground_truth_series: float32 [2048, 128], P('dp'), may hold values from -6 to 6
- valid_len: int32 [128], P('dp'), may hold values from 1 to 16
Outputs:
- input_grads: bfloat16 [32, 2048, 4096], P('section', 'dp')
- down_grads: bfloat16 [32, 4096, 256], P('section', 'dp')
- up_grads: bfloat16 [32, 256, 4096], P('section', None, 'dp')
All inputs are finite; a program needn't handle non-finite values.
Results may differ from a plain program's by a relative error of at most 0.035.
Values may be sent and summed in bfloat16 or wider, within the bound.
A program may use at most 64 MiB of HBM per device.

v0:
```python
import jax
import jax.numpy as jnp
from jax import lax
from jax.sharding import PartitionSpec as P

EPSILON = 1e-05


def from_behind(block, axis, distance):
    devices = range(lax.axis_size(axis))
    route = [(i - distance, i) for i in devices if i - distance in devices]
    return lax.ppermute(block, axis, route)


def normalize(inputs, gain_row):
    values = inputs.astype(jnp.float32)
    inverse = lax.rsqrt(jnp.mean(values * values, axis=-1, keepdims=True) + EPSILON)
    unit = values * inverse
    normed = (unit * gain_row.astype(jnp.float32)).astype(jnp.bfloat16)
    return (inverse, unit, normed)


def multiply_trailing_factor(left, right):
    return lax.dot_general(
        left, right, (((1,), (1,)), ((), ())), preferred_element_type=jnp.float32
    )


def contract_rows(left, right):
    return lax.dot_general(
        left, right, (((0,), (0,)), ((), ())), preferred_element_type=jnp.float32
    )


def block_backward(inverse, unit, latent, gain_row, down_full, up_full, arriving_gradient):
    sigmoid = jax.nn.sigmoid(latent)
    hidden_grad = multiply_trailing_factor(arriving_gradient, up_full)
    latent_grad = (hidden_grad * sigmoid * (1.0 + latent * (1.0 - sigmoid))).astype(jnp.bfloat16)
    scaled = multiply_trailing_factor(latent_grad, down_full) * gain_row.astype(jnp.float32)
    inputs_grad = arriving_gradient.astype(jnp.float32) + inverse * (
        scaled - unit * jnp.mean(scaled * unit, axis=-1, keepdims=True)
    )
    return (inputs_grad.astype(jnp.bfloat16), latent_grad)


def per_device(
    section_inputs, norm_gain, down_proj, up_proj, readout_matrix, ground_truth_series, valid_len
):
    down_full, up_full, entire_readout_matrix = (
        lax.all_gather(down_proj[0], "dp", axis=0, tiled=True),
        lax.all_gather(up_proj[0], "dp", axis=1, tiled=True),
        lax.all_gather(readout_matrix, "dp", axis=0, tiled=True),
    )
    inputs = section_inputs[0]
    gain_row = norm_gain[0]
    microbatch_count = valid_len.shape[0]
    token_count = inputs.shape[0]
    row_count = token_count // microbatch_count
    width = inputs.shape[1]
    latent_width = down_full.shape[1]
    inverse, unit, normed = normalize(inputs, gain_row)
    latent = jnp.dot(normed, down_full, preferred_element_type=jnp.float32)
    activated = jax.nn.silu(latent).astype(jnp.bfloat16)
    section_index = lax.axis_index("section")
    section_last = lax.axis_size("section") - 1
    observed_entry_indicator = (
        (jnp.arange(row_count)[None, :] < valid_len[:, None])
        .astype(jnp.float32)
        .reshape(token_count)
    )

    def loss_grad(unused):
        adapter_output = (
            inputs.astype(jnp.float32)
            + jnp.dot(activated, up_full, preferred_element_type=jnp.float32)
        ).astype(jnp.bfloat16)
        estimated_horizon = jnp.dot(
            adapter_output, entire_readout_matrix, preferred_element_type=jnp.float32
        )
        prediction_discrepancy = (
            observed_entry_indicator[:, None] * (estimated_horizon - ground_truth_series)
        ).astype(jnp.bfloat16)
        return multiply_trailing_factor(prediction_discrepancy, entire_readout_matrix).astype(
            jnp.bfloat16
        )

    def no_loss(unused):
        return jnp.zeros((token_count, width), jnp.bfloat16)

    top_grads = lax.cond(section_index == section_last, loss_grad, no_loss, 0).reshape(
        microbatch_count, row_count, width
    )
    inverse_micro = inverse.reshape(microbatch_count, row_count, 1)
    unit_micro = unit.reshape(microbatch_count, row_count, width)
    latent_micro = latent.reshape(microbatch_count, row_count, latent_width)

    def tick(tick_num, carry):
        outgoing, grads_in, latent_grads, cotangents = carry
        received = from_behind(outgoing, "section", -1)
        micro_num = tick_num - (section_last - section_index)
        is_valid = (micro_num >= 0) & (micro_num < microbatch_count)
        picked = jnp.clip(micro_num, 0, microbatch_count - 1)

        def process(state):
            arrived, grads_prev, latent_prev, cotangent_prev = state
            top_piece = lax.dynamic_index_in_dim(top_grads, picked, 0, keepdims=False)
            arriving_gradient = jnp.where(section_index == section_last, top_piece, arrived)
            inputs_grad, latent_grad = block_backward(
                lax.dynamic_index_in_dim(inverse_micro, picked, 0, keepdims=False),
                lax.dynamic_index_in_dim(unit_micro, picked, 0, keepdims=False),
                lax.dynamic_index_in_dim(latent_micro, picked, 0, keepdims=False),
                gain_row,
                down_full,
                up_full,
                arriving_gradient,
            )
            grads_next = lax.dynamic_update_index_in_dim(grads_prev, inputs_grad, picked, 0)
            latent_next = lax.dynamic_update_index_in_dim(latent_prev, latent_grad, picked, 0)
            cotangent_next = lax.dynamic_update_index_in_dim(
                cotangent_prev, arriving_gradient, picked, 0
            )
            return (inputs_grad, grads_next, latent_next, cotangent_next)

        def skipped(state):
            return state

        return lax.cond(is_valid, process, skipped, (received, grads_in, latent_grads, cotangents))

    initial = (
        jnp.zeros((row_count, width), jnp.bfloat16),
        jnp.zeros((microbatch_count, row_count, width), jnp.bfloat16),
        jnp.zeros((microbatch_count, row_count, latent_width), jnp.bfloat16),
        jnp.zeros((microbatch_count, row_count, width), jnp.bfloat16),
    )
    tick_total = lax.axis_size("section") + microbatch_count - 1
    final_state = lax.fori_loop(0, tick_total, tick, initial)
    grads_in = final_state[1].reshape(1, token_count, width)
    latent_grads = final_state[2].reshape(token_count, latent_width)
    cotangents = final_state[3].reshape(token_count, width)
    down_sum = lax.psum_scatter(
        contract_rows(normed, latent_grads), "dp", scatter_dimension=0, tiled=True
    )
    activated_all = lax.all_gather(activated, "dp", axis=0, tiled=True)
    cotangent_cols = lax.all_to_all(cotangents, "dp", split_axis=1, concat_axis=0, tiled=True)
    up_sum = contract_rows(activated_all, cotangent_cols)
    down_grads = down_sum.astype(jnp.bfloat16)[None]
    up_grads = up_sum.astype(jnp.bfloat16)[None]
    return (grads_in, down_grads, up_grads)


def solution(mesh):
    placed = (
        P("section", "dp", None),
        P("section", None),
        P("section", "dp", None),
        P("section", None, "dp"),
        P("dp", None),
        P("dp", None),
        P("dp"),
    )
    return jax.shard_map(
        per_device,
        mesh=mesh,
        in_specs=placed,
        out_specs=(P("section", "dp", None), P("section", "dp", None), P("section", None, "dp")),
        check_vma=False,
    )
```

profile of v0, /device:TPU:448, one launch (start us, length us, event | category | flops | bytes accessed | tf_op | source)
XLA Modules:
  0.0 932.3 jit_solution(12533757512585029941)
XLA Ops:
  11.8 87.0 %all-gather.11.cloned.1.call-done = bf16[1,4096,256]{2,1,0:T(8,128)(2,1)} async-done(((bf16[1,256,256]{2,1,0:T(8,128)(2,1)}), bf16[1,4096,256]{2,1,0:T(8,128)(2,1)}) %all-gather.11.cloned.1.call-update) | async-done | bytes 2097168 | tf_op jit(solution)/shard_map/all_gather | solution.py:50
  103.7 80.8 %all-gather.7.cloned.1.call-done = bf16[4096,128]{1,0:T(8,128)(2,1)} async-done(((bf16[256,128]{1,0:T(8,128)(2,1)}), bf16[4096,128]{1,0:T(8,128)(2,1)}) %all-gather.7.cloned.1.call-update) | async-done | bytes 1048592 | tf_op jit(solution)/shard_map/all_gather | solution.py:52
  184.5 87.1 %all-gather.13.cloned.1.call-done = bf16[1,256,4096]{2,1,0:T(8,128)(2,1)} async-done(((bf16[1,256,256]{2,1,0:T(8,128)(2,1)}), bf16[1,256,4096]{2,1,0:T(8,128)(2,1)}) %all-gather.13.cloned.1.call-update) | async-done | bytes 2097168 | tf_op jit(solution)/shard_map/all_gather | solution.py:51
  275.1 521.3 %while.20 = (s32[]{:T(128)}, bf16[16,4096]{1,0:T(8,128)(2,1)S(1)}, bf16[8,16,4096]{2,1,0:T(8,128)(2,1)}, bf16[8,16,256]{2,1,0:T(8,128)(2,1)S(1)}, bf16[8,16,4096...) while((s32[]{:T(128)}, bf16[16,4096]{1,0:T(8,128)(2,1)S(1)}, ...), condition=%wide.region_7.8_spmd, body=%wide.region_3.7_spmd.sunk | while | flops 67805192 | bytes 15549357 | solution.py:136
  289.7 7.3 collective-permute-done
  299.0 10.7 %collective-permute-done = bf16[16,4096]{1,0:T(8,128)(2,1)S(1)} collective-permute-done((bf16[16,4096]{1,0:T(8,128)(2,1)S(1)}, bf16[16,4096]{1,0:T(8,128)(2,1)S(1)}, u32[]{:S(2)}, u32[]{:S(2)}) %collective-permute-start) | collective-permute-done | bytes 131104 | tf_op jit(solution)/shard_map/while/body/eval_jaxpr/ppermute | solution.py:12
  311.6 10.6 %collective-permute-done = bf16[16,4096]{1,0:T(8,128)(2,1)S(1)} collective-permute-done((bf16[16,4096]{1,0:T(8,128)(2,1)S(1)}, bf16[16,4096]{1,0:T(8,128)(2,1)S(1)}, u32[]{:S(2)}, u32[]{:S(2)}) %collective-permute-start) | collective-permute-done | bytes 131104 | tf_op jit(solution)/shard_map/while/body/eval_jaxpr/ppermute | solution.py:12
  324.2 10.9 %collective-permute-done = bf16[16,4096]{1,0:T(8,128)(2,1)S(1)} collective-permute-done((bf16[16,4096]{1,0:T(8,128)(2,1)S(1)}, bf16[16,4096]{1,0:T(8,128)(2,1)S(1)}, u32[]{:S(2)}, u32[]{:S(2)}) %collective-permute-start) | collective-permute-done | bytes 131104 | tf_op jit(solution)/shard_map/while/body/eval_jaxpr/ppermute | solution.py:12
  337.0 11.3 %collective-permute-done = bf16[16,4096]{1,0:T(8,128)(2,1)S(1)} collective-permute-done((bf16[16,4096]{1,0:T(8,128)(2,1)S(1)}, bf16[16,4096]{1,0:T(8,128)(2,1)S(1)}, u32[]{:S(2)}, u32[]{:S(2)}) %collective-permute-start) | collective-permute-done | bytes 131104 | tf_op jit(solution)/shard_map/while/body/eval_jaxpr/ppermute | solution.py:12
  350.3 10.7 %collective-permute-done = bf16[16,4096]{1,0:T(8,128)(2,1)S(1)} collective-permute-done((bf16[16,4096]{1,0:T(8,128)(2,1)S(1)}, bf16[16,4096]{1,0:T(8,128)(2,1)S(1)}, u32[]{:S(2)}, u32[]{:S(2)}) %collective-permute-start) | collective-permute-done | bytes 131104 | tf_op jit(solution)/shard_map/while/body/eval_jaxpr/ppermute | solution.py:12
  363.0 10.4 %collective-permute-done = bf16[16,4096]{1,0:T(8,128)(2,1)S(1)} collective-permute-done((bf16[16,4096]{1,0:T(8,128)(2,1)S(1)}, bf16[16,4096]{1,0:T(8,128)(2,1)S(1)}, u32[]{:S(2)}, u32[]{:S(2)}) %collective-permute-start) | collective-permute-done | bytes 131104 | tf_op jit(solution)/shard_map/while/body/eval_jaxpr/ppermute | solution.py:12
  375.4 10.4 %collective-permute-done = bf16[16,4096]{1,0:T(8,128)(2,1)S(1)} collective-permute-done((bf16[16,4096]{1,0:T(8,128)(2,1)S(1)}, bf16[16,4096]{1,0:T(8,128)(2,1)S(1)}, u32[]{:S(2)}, u32[]{:S(2)}) %collective-permute-start) | collective-permute-done | bytes 131104 | tf_op jit(solution)/shard_map/while/body/eval_jaxpr/ppermute | solution.py:12
  387.7 10.4 %collective-permute-done = bf16[16,4096]{1,0:T(8,128)(2,1)S(1)} collective-permute-done((bf16[16,4096]{1,0:T(8,128)(2,1)S(1)}, bf16[16,4096]{1,0:T(8,128)(2,1)S(1)}, u32[]{:S(2)}, u32[]{:S(2)}) %collective-permute-start) | collective-permute-done | bytes 131104 | tf_op jit(solution)/shard_map/while/body/eval_jaxpr/ppermute | solution.py:12
  400.0 10.4 %collective-permute-done = bf16[16,4096]{1,0:T(8,128)(2,1)S(1)} collective-permute-done((bf16[16,4096]{1,0:T(8,128)(2,1)S(1)}, bf16[16,4096]{1,0:T(8,128)(2,1)S(1)}, u32[]{:S(2)}, u32[]{:S(2)}) %collective-permute-start) | collective-permute-done | bytes 131104 | tf_op jit(solution)/shard_map/while/body/eval_jaxpr/ppermute | solution.py:12
  412.4 10.4 %collective-permute-done = bf16[16,4096]{1,0:T(8,128)(2,1)S(1)} collective-permute-done((bf16[16,4096]{1,0:T(8,128)(2,1)S(1)}, bf16[16,4096]{1,0:T(8,128)(2,1)S(1)}, u32[]{:S(2)}, u32[]{:S(2)}) %collective-permute-start) | collective-permute-done | bytes 131104 | tf_op jit(solution)/shard_map/while/body/eval_jaxpr/ppermute | solution.py:12
  424.7 10.4 %collective-permute-done = bf16[16,4096]{1,0:T(8,128)(2,1)S(1)} collective-permute-done((bf16[16,4096]{1,0:T(8,128)(2,1)S(1)}, bf16[16,4096]{1,0:T(8,128)(2,1)S(1)}, u32[]{:S(2)}, u32[]{:S(2)}) %collective-permute-start) | collective-permute-done | bytes 131104 | tf_op jit(solution)/shard_map/while/body/eval_jaxpr/ppermute | solution.py:12
  437.0 10.4 %collective-permute-done = bf16[16,4096]{1,0:T(8,128)(2,1)S(1)} collective-permute-done((bf16[16,4096]{1,0:T(8,128)(2,1)S(1)}, bf16[16,4096]{1,0:T(8,128)(2,1)S(1)}, u32[]{:S(2)}, u32[]{:S(2)}) %collective-permute-start) | collective-permute-done | bytes 131104 | tf_op jit(solution)/shard_map/while/body/eval_jaxpr/ppermute | solution.py:12
  449.4 10.4 %collective-permute-done = bf16[16,4096]{1,0:T(8,128)(2,1)S(1)} collective-permute-done((bf16[16,4096]{1,0:T(8,128)(2,1)S(1)}, bf16[16,4096]{1,0:T(8,128)(2,1)S(1)}, u32[]{:S(2)}, u32[]{:S(2)}) %collective-permute-start) | collective-permute-done | bytes 131104 | tf_op jit(solution)/shard_map/while/body/eval_jaxpr/ppermute | solution.py:12
  461.7 10.4 %collective-permute-done = bf16[16,4096]{1,0:T(8,128)(2,1)S(1)} collective-permute-done((bf16[16,4096]{1,0:T(8,128)(2,1)S(1)}, bf16[16,4096]{1,0:T(8,128)(2,1)S(1)}, u32[]{:S(2)}, u32[]{:S(2)}) %collective-permute-start) | collective-permute-done | bytes 131104 | tf_op jit(solution)/shard_map/while/body/eval_jaxpr/ppermute | solution.py:12
  474.0 17.0 %collective-permute-done = bf16[16,4096]{1,0:T(8,128)(2,1)S(1)} collective-permute-done((bf16[16,4096]{1,0:T(8,128)(2,1)S(1)}, bf16[16,4096]{1,0:T(8,128)(2,1)S(1)}, u32[]{:S(2)}, u32[]{:S(2)}) %collective-permute-start) | collective-permute-done | bytes 131104 | tf_op jit(solution)/shard_map/while/body/eval_jaxpr/ppermute | solution.py:12
  491.0 6.6 conditional.4
  499.6 10.4 %collective-permute-done = bf16[16,4096]{1,0:T(8,128)(2,1)S(1)} collective-permute-done((bf16[16,4096]{1,0:T(8,128)(2,1)S(1)}, bf16[16,4096]{1,0:T(8,128)(2,1)S(1)}, u32[]{:S(2)}, u32[]{:S(2)}) %collective-permute-start) | collective-permute-done | bytes 131104 | tf_op jit(solution)/shard_map/while/body/eval_jaxpr/ppermute | solution.py:12
  518.5 10.4 %collective-permute-done = bf16[16,4096]{1,0:T(8,128)(2,1)S(1)} collective-permute-done((bf16[16,4096]{1,0:T(8,128)(2,1)S(1)}, bf16[16,4096]{1,0:T(8,128)(2,1)S(1)}, u32[]{:S(2)}, u32[]{:S(2)}) %collective-permute-start) | collective-permute-done | bytes 131104 | tf_op jit(solution)/shard_map/while/body/eval_jaxpr/ppermute | solution.py:12
  528.9 6.6 conditional.4
  537.5 10.4 %collective-permute-done = bf16[16,4096]{1,0:T(8,128)(2,1)S(1)} collective-permute-done((bf16[16,4096]{1,0:T(8,128)(2,1)S(1)}, bf16[16,4096]{1,0:T(8,128)(2,1)S(1)}, u32[]{:S(2)}, u32[]{:S(2)}) %collective-permute-start) | collective-permute-done | bytes 131104 | tf_op jit(solution)/shard_map/while/body/eval_jaxpr/ppermute | solution.py:12
  547.8 6.6 conditional.4
  556.4 10.4 %collective-permute-done = bf16[16,4096]{1,0:T(8,128)(2,1)S(1)} collective-permute-done((bf16[16,4096]{1,0:T(8,128)(2,1)S(1)}, bf16[16,4096]{1,0:T(8,128)(2,1)S(1)}, u32[]{:S(2)}, u32[]{:S(2)}) %collective-permute-start) | collective-permute-done | bytes 131104 | tf_op jit(solution)/shard_map/while/body/eval_jaxpr/ppermute | solution.py:12
  566.8 6.6 conditional.4
  575.4 10.3 %collective-permute-done = bf16[16,4096]{1,0:T(8,128)(2,1)S(1)} collective-permute-done((bf16[16,4096]{1,0:T(8,128)(2,1)S(1)}, bf16[16,4096]{1,0:T(8,128)(2,1)S(1)}, u32[]{:S(2)}, u32[]{:S(2)}) %collective-permute-start) | collective-permute-done | bytes 131104 | tf_op jit(solution)/shard_map/while/body/eval_jaxpr/ppermute | solution.py:12
  585.8 6.6 conditional.4
  594.4 10.3 %collective-permute-done = bf16[16,4096]{1,0:T(8,128)(2,1)S(1)} collective-permute-done((bf16[16,4096]{1,0:T(8,128)(2,1)S(1)}, bf16[16,4096]{1,0:T(8,128)(2,1)S(1)}, u32[]{:S(2)}, u32[]{:S(2)}) %collective-permute-start) | collective-permute-done | bytes 131104 | tf_op jit(solution)/shard_map/while/body/eval_jaxpr/ppermute | solution.py:12
  613.3 10.4 %collective-permute-done = bf16[16,4096]{1,0:T(8,128)(2,1)S(1)} collective-permute-done((bf16[16,4096]{1,0:T(8,128)(2,1)S(1)}, bf16[16,4096]{1,0:T(8,128)(2,1)S(1)}, u32[]{:S(2)}, u32[]{:S(2)}) %collective-permute-start) | collective-permute-done | bytes 131104 | tf_op jit(solution)/shard_map/while/body/eval_jaxpr/ppermute | solution.py:12
  623.7 6.6 conditional.4
  636.0 9.1 collective-permute-start
  651.5 9.2 collective-permute-done
  662.6 10.4 %collective-permute-done = bf16[16,4096]{1,0:T(8,128)(2,1)S(1)} collective-permute-done((bf16[16,4096]{1,0:T(8,128)(2,1)S(1)}, bf16[16,4096]{1,0:T(8,128)(2,1)S(1)}, u32[]{:S(2)}, u32[]{:S(2)}) %collective-permute-start) | collective-permute-done | bytes 131104 | tf_op jit(solution)/shard_map/while/body/eval_jaxpr/ppermute | solution.py:12
  675.0 10.4 %collective-permute-done = bf16[16,4096]{1,0:T(8,128)(2,1)S(1)} collective-permute-done((bf16[16,4096]{1,0:T(8,128)(2,1)S(1)}, bf16[16,4096]{1,0:T(8,128)(2,1)S(1)}, u32[]{:S(2)}, u32[]{:S(2)}) %collective-permute-start) | collective-permute-done | bytes 131104 | tf_op jit(solution)/shard_map/while/body/eval_jaxpr/ppermute | solution.py:12
  687.3 10.4 %collective-permute-done = bf16[16,4096]{1,0:T(8,128)(2,1)S(1)} collective-permute-done((bf16[16,4096]{1,0:T(8,128)(2,1)S(1)}, bf16[16,4096]{1,0:T(8,128)(2,1)S(1)}, u32[]{:S(2)}, u32[]{:S(2)}) %collective-permute-start) | collective-permute-done | bytes 131104 | tf_op jit(solution)/shard_map/while/body/eval_jaxpr/ppermute | solution.py:12
  699.6 10.4 %collective-permute-done = bf16[16,4096]{1,0:T(8,128)(2,1)S(1)} collective-permute-done((bf16[16,4096]{1,0:T(8,128)(2,1)S(1)}, bf16[16,4096]{1,0:T(8,128)(2,1)S(1)}, u32[]{:S(2)}, u32[]{:S(2)}) %collective-permute-start) | collective-permute-done | bytes 131104 | tf_op jit(solution)/shard_map/while/body/eval_jaxpr/ppermute | solution.py:12
  712.0 10.4 %collective-permute-done = bf16[16,4096]{1,0:T(8,128)(2,1)S(1)} collective-permute-done((bf16[16,4096]{1,0:T(8,128)(2,1)S(1)}, bf16[16,4096]{1,0:T(8,128)(2,1)S(1)}, u32[]{:S(2)}, u32[]{:S(2)}) %collective-permute-start) | collective-permute-done | bytes 131104 | tf_op jit(solution)/shard_map/while/body/eval_jaxpr/ppermute | solution.py:12
  724.3 10.4 %collective-permute-done = bf16[16,4096]{1,0:T(8,128)(2,1)S(1)} collective-permute-done((bf16[16,4096]{1,0:T(8,128)(2,1)S(1)}, bf16[16,4096]{1,0:T(8,128)(2,1)S(1)}, u32[]{:S(2)}, u32[]{:S(2)}) %collective-permute-start) | collective-permute-done | bytes 131104 | tf_op jit(solution)/shard_map/while/body/eval_jaxpr/ppermute | solution.py:12
  736.6 10.4 %collective-permute-done = bf16[16,4096]{1,0:T(8,128)(2,1)S(1)} collective-permute-done((bf16[16,4096]{1,0:T(8,128)(2,1)S(1)}, bf16[16,4096]{1,0:T(8,128)(2,1)S(1)}, u32[]{:S(2)}, u32[]{:S(2)}) %collective-permute-start) | collective-permute-done | bytes 131104 | tf_op jit(solution)/shard_map/while/body/eval_jaxpr/ppermute | solution.py:12
  749.0 10.4 %collective-permute-done = bf16[16,4096]{1,0:T(8,128)(2,1)S(1)} collective-permute-done((bf16[16,4096]{1,0:T(8,128)(2,1)S(1)}, bf16[16,4096]{1,0:T(8,128)(2,1)S(1)}, u32[]{:S(2)}, u32[]{:S(2)}) %collective-permute-start) | collective-permute-done | bytes 131104 | tf_op jit(solution)/shard_map/while/body/eval_jaxpr/ppermute | solution.py:12
  761.3 10.4 %collective-permute-done = bf16[16,4096]{1,0:T(8,128)(2,1)S(1)} collective-permute-done((bf16[16,4096]{1,0:T(8,128)(2,1)S(1)}, bf16[16,4096]{1,0:T(8,128)(2,1)S(1)}, u32[]{:S(2)}, u32[]{:S(2)}) %collective-permute-start) | collective-permute-done | bytes 131104 | tf_op jit(solution)/shard_map/while/body/eval_jaxpr/ppermute | solution.py:12
  773.6 10.4 %collective-permute-done = bf16[16,4096]{1,0:T(8,128)(2,1)S(1)} collective-permute-done((bf16[16,4096]{1,0:T(8,128)(2,1)S(1)}, bf16[16,4096]{1,0:T(8,128)(2,1)S(1)}, u32[]{:S(2)}, u32[]{:S(2)}) %collective-permute-start) | collective-permute-done | bytes 131104 | tf_op jit(solution)/shard_map/while/body/eval_jaxpr/ppermute | solution.py:12
  786.0 10.4 %collective-permute-done = bf16[16,4096]{1,0:T(8,128)(2,1)S(1)} collective-permute-done((bf16[16,4096]{1,0:T(8,128)(2,1)S(1)}, bf16[16,4096]{1,0:T(8,128)(2,1)S(1)}, u32[]{:S(2)}, u32[]{:S(2)}) %collective-permute-start) | collective-permute-done | bytes 131104 | tf_op jit(solution)/shard_map/while/body/eval_jaxpr/ppermute | solution.py:12
  801.0 43.8 %all_to_all.19 = bf16[128,16,256]{2,0,1:T(8,128)(2,1)S(1)} all-to-all(bf16[128,16,256]{2,0,1:T(8,128)(2,1)S(1)} %copy.16), channel_id=1, replica_groups=mesh['section'=32,'dp'=16] {'dp'}, dimensions={1} | all-to-all | bytes 2097152 | tf_op jit(solution)/shard_map/all_to_all | solution.py:144
  847.1 77.1 %reduce-scatter.2.cloned.1.call-done = f32[256,256]{1,0:T(8,128)} async-done(((f32[4096,256]{1,0:T(8,128)}), f32[256,256]{1,0:T(8,128)}) %reduce-scatter.2.cloned.1.call-update) | async-done | bytes 262160 | tf_op jit(solution)/shard_map/reduce_scatter | solution.py:140
  (229 shorter events, 178.5 us)
Async XLA Ops:
  7.2 91.6 %all-gather.11.cloned.1.call-start = ((), (), s32[]{:S(2)}) async-start(), calls=%async_computation.5 | async-start | bytes 2228224 | tf_op jit(solution)/shard_map/all_gather | solution.py:50
  7.9 176.6 %all-gather.7.cloned.1.call-start = ((), (), s32[]{:S(2)}) async-start(), calls=%async_computation.2 | async-start | bytes 1114112 | tf_op jit(solution)/shard_map/all_gather | solution.py:52
  8.6 263.0 %all-gather.13.cloned.1.call-start = ((), (), s32[]{:S(2)}) async-start(), calls=%async_computation.6 | async-start | bytes 2228224 | tf_op jit(solution)/shard_map/all_gather | solution.py:51
  9.4 835.3 %all-gather.9.cloned.1.call-start = ((), (), s32[]{:S(2)}) async-start(), calls=%async_computation.4 | async-start | bytes 1114112 | tf_op jit(solution)/shard_map/all_gather | solution.py:143
  11.7 90.4 %copy-start.7 = (s32[8]{0:T(128)S(1)}, s32[8]{0:T(128)}, u32[]{:S(2)}) copy-start(s32[8]{0:T(128)} %param.19) | copy-start | bytes 100
  11.7 90.4 %copy-start.2 = (bf16[1,128,4096]{2,1,0:T(8,128)(2,1)S(1)}, bf16[1,128,4096]{2,1,0:T(8,128)(2,1)}, u32[]{:S(2)}) copy-start(bf16[1,128,4096]{2,1,0:T(8,128)(2,1)} %param.13) | copy-start | bytes 3145732
  101.9 169.8 %copy-start.5 = (bf16[128,256]{1,0:T(8,128)(2,1)S(1)}, bf16[128,256]{1,0:T(8,128)(2,1)}, u32[]{:S(2)}) copy-start(bf16[128,256]{1,0:T(8,128)(2,1)} %get-tuple-element.490) | copy-start | bytes 196612
  101.9 169.8 %copy-start.6 = (f32[128,128]{1,0:T(8,128)S(1)}, f32[128,128]{1,0:T(8,128)}, u32[]{:S(2)}) copy-start(f32[128,128]{1,0:T(8,128)} %param.18) | copy-start | bytes 196612
  101.9 822.3 %reduce-scatter.2.cloned.1.call-start = ((), (), s32[]{:S(2)}) async-start(), calls=%async_computation.3 | async-start | bytes 4456448 | tf_op jit(solution)/shard_map/reduce_scatter | solution.py:140
  275.1 4.4 collective-permute-start
  279.6 6.3 collective-permute-start
  285.9 11.1 %collective-permute-start = (bf16[16,4096]{1,0:T(8,128)(2,1)S(1)}, bf16[16,4096]{1,0:T(8,128)(2,1)S(1)}, u32[]{:S(2)}, u32[]{:S(2)}) collective-permute-start(bf16[16,4096]{1,0:T(8,128)(2,1)S(1)} %get-tuple-element.611), channel_id=1, source_target_pairs={{16,0},{32,16},{48,32},{64,48},{80,64},{96,80},{112,96},{128,112},... | collective-permute-start | bytes 393224 | tf_op jit(solution)/shard_map/while/body/eval_jaxpr/ppermute | solution.py:12
  297.0 12.7 %collective-permute-start = (bf16[16,4096]{1,0:T(8,128)(2,1)S(1)}, bf16[16,4096]{1,0:T(8,128)(2,1)S(1)}, u32[]{:S(2)}, u32[]{:S(2)}) collective-permute-start(bf16[16,4096]{1,0:T(8,128)(2,1)S(1)} %get-tuple-element.611), channel_id=1, source_target_pairs={{16,0},{32,16},{48,32},{64,48},{80,64},{96,80},{112,96},{128,112},... | collective-permute-start | bytes 393224 | tf_op jit(solution)/shard_map/while/body/eval_jaxpr/ppermute | solution.py:12
  309.7 12.5 %collective-permute-start = (bf16[16,4096]{1,0:T(8,128)(2,1)S(1)}, bf16[16,4096]{1,0:T(8,128)(2,1)S(1)}, u32[]{:S(2)}, u32[]{:S(2)}) collective-permute-start(bf16[16,4096]{1,0:T(8,128)(2,1)S(1)} %get-tuple-element.611), channel_id=1, source_target_pairs={{16,0},{32,16},{48,32},{64,48},{80,64},{96,80},{112,96},{128,112},... | collective-permute-start | bytes 393224 | tf_op jit(solution)/shard_map/while/body/eval_jaxpr/ppermute | solution.py:12
  322.2 12.8 %collective-permute-start = (bf16[16,4096]{1,0:T(8,128)(2,1)S(1)}, bf16[16,4096]{1,0:T(8,128)(2,1)S(1)}, u32[]{:S(2)}, u32[]{:S(2)}) collective-permute-start(bf16[16,4096]{1,0:T(8,128)(2,1)S(1)} %get-tuple-element.611), channel_id=1, source_target_pairs={{16,0},{32,16},{48,32},{64,48},{80,64},{96,80},{112,96},{128,112},... | collective-permute-start | bytes 393224 | tf_op jit(solution)/shard_map/while/body/eval_jaxpr/ppermute | solution.py:12
  335.1 13.3 %collective-permute-start = (bf16[16,4096]{1,0:T(8,128)(2,1)S(1)}, bf16[16,4096]{1,0:T(8,128)(2,1)S(1)}, u32[]{:S(2)}, u32[]{:S(2)}) collective-permute-start(bf16[16,4096]{1,0:T(8,128)(2,1)S(1)} %get-tuple-element.611), channel_id=1, source_target_pairs={{16,0},{32,16},{48,32},{64,48},{80,64},{96,80},{112,96},{128,112},... | collective-permute-start | bytes 393224 | tf_op jit(solution)/shard_map/while/body/eval_jaxpr/ppermute | solution.py:12
  348.4 12.7 %collective-permute-start = (bf16[16,4096]{1,0:T(8,128)(2,1)S(1)}, bf16[16,4096]{1,0:T(8,128)(2,1)S(1)}, u32[]{:S(2)}, u32[]{:S(2)}) collective-permute-start(bf16[16,4096]{1,0:T(8,128)(2,1)S(1)} %get-tuple-element.611), channel_id=1, source_target_pairs={{16,0},{32,16},{48,32},{64,48},{80,64},{96,80},{112,96},{128,112},... | collective-permute-start | bytes 393224 | tf_op jit(solution)/shard_map/while/body/eval_jaxpr/ppermute | solution.py:12
  361.1 12.3 %collective-permute-start = (bf16[16,4096]{1,0:T(8,128)(2,1)S(1)}, bf16[16,4096]{1,0:T(8,128)(2,1)S(1)}, u32[]{:S(2)}, u32[]{:S(2)}) collective-permute-start(bf16[16,4096]{1,0:T(8,128)(2,1)S(1)} %get-tuple-element.611), channel_id=1, source_target_pairs={{16,0},{32,16},{48,32},{64,48},{80,64},{96,80},{112,96},{128,112},... | collective-permute-start | bytes 393224 | tf_op jit(solution)/shard_map/while/body/eval_jaxpr/ppermute | solution.py:12
  373.4 12.3 %collective-permute-start = (bf16[16,4096]{1,0:T(8,128)(2,1)S(1)}, bf16[16,4096]{1,0:T(8,128)(2,1)S(1)}, u32[]{:S(2)}, u32[]{:S(2)}) collective-permute-start(bf16[16,4096]{1,0:T(8,128)(2,1)S(1)} %get-tuple-element.611), channel_id=1, source_target_pairs={{16,0},{32,16},{48,32},{64,48},{80,64},{96,80},{112,96},{128,112},... | collective-permute-start | bytes 393224 | tf_op jit(solution)/shard_map/while/body/eval_jaxpr/ppermute | solution.py:12
  385.8 12.3 %collective-permute-start = (bf16[16,4096]{1,0:T(8,128)(2,1)S(1)}, bf16[16,4096]{1,0:T(8,128)(2,1)S(1)}, u32[]{:S(2)}, u32[]{:S(2)}) collective-permute-start(bf16[16,4096]{1,0:T(8,128)(2,1)S(1)} %get-tuple-element.611), channel_id=1, source_target_pairs={{16,0},{32,16},{48,32},{64,48},{80,64},{96,80},{112,96},{128,112},... | collective-permute-start | bytes 393224 | tf_op jit(solution)/shard_map/while/body/eval_jaxpr/ppermute | solution.py:12
  398.1 12.3 %collective-permute-start = (bf16[16,4096]{1,0:T(8,128)(2,1)S(1)}, bf16[16,4096]{1,0:T(8,128)(2,1)S(1)}, u32[]{:S(2)}, u32[]{:S(2)}) collective-permute-start(bf16[16,4096]{1,0:T(8,128)(2,1)S(1)} %get-tuple-element.611), channel_id=1, source_target_pairs={{16,0},{32,16},{48,32},{64,48},{80,64},{96,80},{112,96},{128,112},... | collective-permute-start | bytes 393224 | tf_op jit(solution)/shard_map/while/body/eval_jaxpr/ppermute | solution.py:12
  410.4 12.3 %collective-permute-start = (bf16[16,4096]{1,0:T(8,128)(2,1)S(1)}, bf16[16,4096]{1,0:T(8,128)(2,1)S(1)}, u32[]{:S(2)}, u32[]{:S(2)}) collective-permute-start(bf16[16,4096]{1,0:T(8,128)(2,1)S(1)} %get-tuple-element.611), channel_id=1, source_target_pairs={{16,0},{32,16},{48,32},{64,48},{80,64},{96,80},{112,96},{128,112},... | collective-permute-start | bytes 393224 | tf_op jit(solution)/shard_map/while/body/eval_jaxpr/ppermute | solution.py:12
  422.8 12.3 %collective-permute-start = (bf16[16,4096]{1,0:T(8,128)(2,1)S(1)}, bf16[16,4096]{1,0:T(8,128)(2,1)S(1)}, u32[]{:S(2)}, u32[]{:S(2)}) collective-permute-start(bf16[16,4096]{1,0:T(8,128)(2,1)S(1)} %get-tuple-element.611), channel_id=1, source_target_pairs={{16,0},{32,16},{48,32},{64,48},{80,64},{96,80},{112,96},{128,112},... | collective-permute-start | bytes 393224 | tf_op jit(solution)/shard_map/while/body/eval_jaxpr/ppermute | solution.py:12
  435.1 12.3 %collective-permute-start = (bf16[16,4096]{1,0:T(8,128)(2,1)S(1)}, bf16[16,4096]{1,0:T(8,128)(2,1)S(1)}, u32[]{:S(2)}, u32[]{:S(2)}) collective-permute-start(bf16[16,4096]{1,0:T(8,128)(2,1)S(1)} %get-tuple-element.611), channel_id=1, source_target_pairs={{16,0},{32,16},{48,32},{64,48},{80,64},{96,80},{112,96},{128,112},... | collective-permute-start | bytes 393224 | tf_op jit(solution)/shard_map/while/body/eval_jaxpr/ppermute | solution.py:12
  447.4 12.3 %collective-permute-start = (bf16[16,4096]{1,0:T(8,128)(2,1)S(1)}, bf16[16,4096]{1,0:T(8,128)(2,1)S(1)}, u32[]{:S(2)}, u32[]{:S(2)}) collective-permute-start(bf16[16,4096]{1,0:T(8,128)(2,1)S(1)} %get-tuple-element.611), channel_id=1, source_target_pairs={{16,0},{32,16},{48,32},{64,48},{80,64},{96,80},{112,96},{128,112},... | collective-permute-start | bytes 393224 | tf_op jit(solution)/shard_map/while/body/eval_jaxpr/ppermute | solution.py:12
  459.8 12.3 %collective-permute-start = (bf16[16,4096]{1,0:T(8,128)(2,1)S(1)}, bf16[16,4096]{1,0:T(8,128)(2,1)S(1)}, u32[]{:S(2)}, u32[]{:S(2)}) collective-permute-start(bf16[16,4096]{1,0:T(8,128)(2,1)S(1)} %get-tuple-element.611), channel_id=1, source_target_pairs={{16,0},{32,16},{48,32},{64,48},{80,64},{96,80},{112,96},{128,112},... | collective-permute-start | bytes 393224 | tf_op jit(solution)/shard_map/while/body/eval_jaxpr/ppermute | solution.py:12
  472.1 18.9 %collective-permute-start = (bf16[16,4096]{1,0:T(8,128)(2,1)S(1)}, bf16[16,4096]{1,0:T(8,128)(2,1)S(1)}, u32[]{:S(2)}, u32[]{:S(2)}) collective-permute-start(bf16[16,4096]{1,0:T(8,128)(2,1)S(1)} %get-tuple-element.611), channel_id=1, source_target_pairs={{16,0},{32,16},{48,32},{64,48},{80,64},{96,80},{112,96},{128,112},... | collective-permute-start | bytes 393224 | tf_op jit(solution)/shard_map/while/body/eval_jaxpr/ppermute | solution.py:12
  497.7 12.3 %collective-permute-start = (bf16[16,4096]{1,0:T(8,128)(2,1)S(1)}, bf16[16,4096]{1,0:T(8,128)(2,1)S(1)}, u32[]{:S(2)}, u32[]{:S(2)}) collective-permute-start(bf16[16,4096]{1,0:T(8,128)(2,1)S(1)} %get-tuple-element.611), channel_id=1, source_target_pairs={{16,0},{32,16},{48,32},{64,48},{80,64},{96,80},{112,96},{128,112},... | collective-permute-start | bytes 393224 | tf_op jit(solution)/shard_map/while/body/eval_jaxpr/ppermute | solution.py:12
  516.6 12.3 %collective-permute-start = (bf16[16,4096]{1,0:T(8,128)(2,1)S(1)}, bf16[16,4096]{1,0:T(8,128)(2,1)S(1)}, u32[]{:S(2)}, u32[]{:S(2)}) collective-permute-start(bf16[16,4096]{1,0:T(8,128)(2,1)S(1)} %get-tuple-element.611), channel_id=1, source_target_pairs={{16,0},{32,16},{48,32},{64,48},{80,64},{96,80},{112,96},{128,112},... | collective-permute-start | bytes 393224 | tf_op jit(solution)/shard_map/while/body/eval_jaxpr/ppermute | solution.py:12
  535.5 12.3 %collective-permute-start = (bf16[16,4096]{1,0:T(8,128)(2,1)S(1)}, bf16[16,4096]{1,0:T(8,128)(2,1)S(1)}, u32[]{:S(2)}, u32[]{:S(2)}) collective-permute-start(bf16[16,4096]{1,0:T(8,128)(2,1)S(1)} %get-tuple-element.611), channel_id=1, source_target_pairs={{16,0},{32,16},{48,32},{64,48},{80,64},{96,80},{112,96},{128,112},... | collective-permute-start | bytes 393224 | tf_op jit(solution)/shard_map/while/body/eval_jaxpr/ppermute | solution.py:12
  554.5 12.3 %collective-permute-start = (bf16[16,4096]{1,0:T(8,128)(2,1)S(1)}, bf16[16,4096]{1,0:T(8,128)(2,1)S(1)}, u32[]{:S(2)}, u32[]{:S(2)}) collective-permute-start(bf16[16,4096]{1,0:T(8,128)(2,1)S(1)} %get-tuple-element.611), channel_id=1, source_target_pairs={{16,0},{32,16},{48,32},{64,48},{80,64},{96,80},{112,96},{128,112},... | collective-permute-start | bytes 393224 | tf_op jit(solution)/shard_map/while/body/eval_jaxpr/ppermute | solution.py:12
  573.5 12.3 %collective-permute-start = (bf16[16,4096]{1,0:T(8,128)(2,1)S(1)}, bf16[16,4096]{1,0:T(8,128)(2,1)S(1)}, u32[]{:S(2)}, u32[]{:S(2)}) collective-permute-start(bf16[16,4096]{1,0:T(8,128)(2,1)S(1)} %get-tuple-element.611), channel_id=1, source_target_pairs={{16,0},{32,16},{48,32},{64,48},{80,64},{96,80},{112,96},{128,112},... | collective-permute-start | bytes 393224 | tf_op jit(solution)/shard_map/while/body/eval_jaxpr/ppermute | solution.py:12
  592.4 12.3 %collective-permute-start = (bf16[16,4096]{1,0:T(8,128)(2,1)S(1)}, bf16[16,4096]{1,0:T(8,128)(2,1)S(1)}, u32[]{:S(2)}, u32[]{:S(2)}) collective-permute-start(bf16[16,4096]{1,0:T(8,128)(2,1)S(1)} %get-tuple-element.611), channel_id=1, source_target_pairs={{16,0},{32,16},{48,32},{64,48},{80,64},{96,80},{112,96},{128,112},... | collective-permute-start | bytes 393224 | tf_op jit(solution)/shard_map/while/body/eval_jaxpr/ppermute | solution.py:12
  611.3 12.3 %collective-permute-start = (bf16[16,4096]{1,0:T(8,128)(2,1)S(1)}, bf16[16,4096]{1,0:T(8,128)(2,1)S(1)}, u32[]{:S(2)}, u32[]{:S(2)}) collective-permute-start(bf16[16,4096]{1,0:T(8,128)(2,1)S(1)} %get-tuple-element.611), channel_id=1, source_target_pairs={{16,0},{32,16},{48,32},{64,48},{80,64},{96,80},{112,96},{128,112},... | collective-permute-start | bytes 393224 | tf_op jit(solution)/shard_map/while/body/eval_jaxpr/ppermute | solution.py:12
  630.3 5.7 collective-permute-start
  636.0 12.3 %collective-permute-start = (bf16[16,4096]{1,0:T(8,128)(2,1)S(1)}, bf16[16,4096]{1,0:T(8,128)(2,1)S(1)}, u32[]{:S(2)}, u32[]{:S(2)}) collective-permute-start(bf16[16,4096]{1,0:T(8,128)(2,1)S(1)} %get-tuple-element.611), channel_id=1, source_target_pairs={{16,0},{32,16},{48,32},{64,48},{80,64},{96,80},{112,96},{128,112},... | collective-permute-start | bytes 393224 | tf_op jit(solution)/shard_map/while/body/eval_jaxpr/ppermute | solution.py:12
  648.4 12.3 %collective-permute-start = (bf16[16,4096]{1,0:T(8,128)(2,1)S(1)}, bf16[16,4096]{1,0:T(8,128)(2,1)S(1)}, u32[]{:S(2)}, u32[]{:S(2)}) collective-permute-start(bf16[16,4096]{1,0:T(8,128)(2,1)S(1)} %get-tuple-element.611), channel_id=1, source_target_pairs={{16,0},{32,16},{48,32},{64,48},{80,64},{96,80},{112,96},{128,112},... | collective-permute-start | bytes 393224 | tf_op jit(solution)/shard_map/while/body/eval_jaxpr/ppermute | solution.py:12
  660.7 12.3 %collective-permute-start = (bf16[16,4096]{1,0:T(8,128)(2,1)S(1)}, bf16[16,4096]{1,0:T(8,128)(2,1)S(1)}, u32[]{:S(2)}, u32[]{:S(2)}) collective-permute-start(bf16[16,4096]{1,0:T(8,128)(2,1)S(1)} %get-tuple-element.611), channel_id=1, source_target_pairs={{16,0},{32,16},{48,32},{64,48},{80,64},{96,80},{112,96},{128,112},... | collective-permute-start | bytes 393224 | tf_op jit(solution)/shard_map/while/body/eval_jaxpr/ppermute | solution.py:12
  673.0 12.3 %collective-permute-start = (bf16[16,4096]{1,0:T(8,128)(2,1)S(1)}, bf16[16,4096]{1,0:T(8,128)(2,1)S(1)}, u32[]{:S(2)}, u32[]{:S(2)}) collective-permute-start(bf16[16,4096]{1,0:T(8,128)(2,1)S(1)} %get-tuple-element.611), channel_id=1, source_target_pairs={{16,0},{32,16},{48,32},{64,48},{80,64},{96,80},{112,96},{128,112},... | collective-permute-start | bytes 393224 | tf_op jit(solution)/shard_map/while/body/eval_jaxpr/ppermute | solution.py:12
  685.4 12.3 %collective-permute-start = (bf16[16,4096]{1,0:T(8,128)(2,1)S(1)}, bf16[16,4096]{1,0:T(8,128)(2,1)S(1)}, u32[]{:S(2)}, u32[]{:S(2)}) collective-permute-start(bf16[16,4096]{1,0:T(8,128)(2,1)S(1)} %get-tuple-element.611), channel_id=1, source_target_pairs={{16,0},{32,16},{48,32},{64,48},{80,64},{96,80},{112,96},{128,112},... | collective-permute-start | bytes 393224 | tf_op jit(solution)/shard_map/while/body/eval_jaxpr/ppermute | solution.py:12
  697.7 12.3 %collective-permute-start = (bf16[16,4096]{1,0:T(8,128)(2,1)S(1)}, bf16[16,4096]{1,0:T(8,128)(2,1)S(1)}, u32[]{:S(2)}, u32[]{:S(2)}) collective-permute-start(bf16[16,4096]{1,0:T(8,128)(2,1)S(1)} %get-tuple-element.611), channel_id=1, source_target_pairs={{16,0},{32,16},{48,32},{64,48},{80,64},{96,80},{112,96},{128,112},... | collective-permute-start | bytes 393224 | tf_op jit(solution)/shard_map/while/body/eval_jaxpr/ppermute | solution.py:12
  710.0 12.3 %collective-permute-start = (bf16[16,4096]{1,0:T(8,128)(2,1)S(1)}, bf16[16,4096]{1,0:T(8,128)(2,1)S(1)}, u32[]{:S(2)}, u32[]{:S(2)}) collective-permute-start(bf16[16,4096]{1,0:T(8,128)(2,1)S(1)} %get-tuple-element.611), channel_id=1, source_target_pairs={{16,0},{32,16},{48,32},{64,48},{80,64},{96,80},{112,96},{128,112},... | collective-permute-start | bytes 393224 | tf_op jit(solution)/shard_map/while/body/eval_jaxpr/ppermute | solution.py:12
  722.4 12.3 %collective-permute-start = (bf16[16,4096]{1,0:T(8,128)(2,1)S(1)}, bf16[16,4096]{1,0:T(8,128)(2,1)S(1)}, u32[]{:S(2)}, u32[]{:S(2)}) collective-permute-start(bf16[16,4096]{1,0:T(8,128)(2,1)S(1)} %get-tuple-element.611), channel_id=1, source_target_pairs={{16,0},{32,16},{48,32},{64,48},{80,64},{96,80},{112,96},{128,112},... | collective-permute-start | bytes 393224 | tf_op jit(solution)/shard_map/while/body/eval_jaxpr/ppermute | solution.py:12
  734.7 12.3 %collective-permute-start = (bf16[16,4096]{1,0:T(8,128)(2,1)S(1)}, bf16[16,4096]{1,0:T(8,128)(2,1)S(1)}, u32[]{:S(2)}, u32[]{:S(2)}) collective-permute-start(bf16[16,4096]{1,0:T(8,128)(2,1)S(1)} %get-tuple-element.611), channel_id=1, source_target_pairs={{16,0},{32,16},{48,32},{64,48},{80,64},{96,80},{112,96},{128,112},... | collective-permute-start | bytes 393224 | tf_op jit(solution)/shard_map/while/body/eval_jaxpr/ppermute | solution.py:12
  747.0 12.3 %collective-permute-start = (bf16[16,4096]{1,0:T(8,128)(2,1)S(1)}, bf16[16,4096]{1,0:T(8,128)(2,1)S(1)}, u32[]{:S(2)}, u32[]{:S(2)}) collective-permute-start(bf16[16,4096]{1,0:T(8,128)(2,1)S(1)} %get-tuple-element.611), channel_id=1, source_target_pairs={{16,0},{32,16},{48,32},{64,48},{80,64},{96,80},{112,96},{128,112},... | collective-permute-start | bytes 393224 | tf_op jit(solution)/shard_map/while/body/eval_jaxpr/ppermute | solution.py:12
  759.4 12.3 %collective-permute-start = (bf16[16,4096]{1,0:T(8,128)(2,1)S(1)}, bf16[16,4096]{1,0:T(8,128)(2,1)S(1)}, u32[]{:S(2)}, u32[]{:S(2)}) collective-permute-start(bf16[16,4096]{1,0:T(8,128)(2,1)S(1)} %get-tuple-element.611), channel_id=1, source_target_pairs={{16,0},{32,16},{48,32},{64,48},{80,64},{96,80},{112,96},{128,112},... | collective-permute-start | bytes 393224 | tf_op jit(solution)/shard_map/while/body/eval_jaxpr/ppermute | solution.py:12
  771.7 12.3 %collective-permute-start = (bf16[16,4096]{1,0:T(8,128)(2,1)S(1)}, bf16[16,4096]{1,0:T(8,128)(2,1)S(1)}, u32[]{:S(2)}, u32[]{:S(2)}) collective-permute-start(bf16[16,4096]{1,0:T(8,128)(2,1)S(1)} %get-tuple-element.611), channel_id=1, source_target_pairs={{16,0},{32,16},{48,32},{64,48},{80,64},{96,80},{112,96},{128,112},... | collective-permute-start | bytes 393224 | tf_op jit(solution)/shard_map/while/body/eval_jaxpr/ppermute | solution.py:12
  784.0 12.3 %collective-permute-start = (bf16[16,4096]{1,0:T(8,128)(2,1)S(1)}, bf16[16,4096]{1,0:T(8,128)(2,1)S(1)}, u32[]{:S(2)}, u32[]{:S(2)}) collective-permute-start(bf16[16,4096]{1,0:T(8,128)(2,1)S(1)} %get-tuple-element.611), channel_id=1, source_target_pairs={{16,0},{32,16},{48,32},{64,48},{80,64},{96,80},{112,96},{128,112},... | collective-permute-start | bytes 393224 | tf_op jit(solution)/shard_map/while/body/eval_jaxpr/ppermute | solution.py:12
  (10 other events, 28.5 us)
Sparse Core Ops, SparseCore 0:
  10.1 88.6 all-gather.10
  100.9 83.6 all-gather.6
  186.5 85.0 all-gather.12
  274.2 83.3 all-gather.8
  799.3 124.8 reduce-scatter.1
where the time goes:
time: 935 us; the launch traced here: 932 us
  waiting for transfers between devices  714 us (76%)
  starting transfers between devices  87.2 us (9%)
  blocking collectives  43.8 us (5%)
  other arithmetic  33.4 us (4%)
  matrix products  32.9 us (4%)
  between operations  13.8 us (1%)
    ppermute x39, waiting for transfers between devices, from_behind(): return lax.ppermute(block, axis, route)  379 us
    all_gather x1, waiting for transfers between devices, per_device(): lax.all_gather(up_proj[0], 'dp', axis=1, tiled=True)  87.1 us
    ppermute x39, starting transfers between devices, from_behind(): return lax.ppermute(block, axis, route)  87 us
    all_gather x1, waiting for transfers between devices, per_device(): lax.all_gather(down_proj[0], 'dp', axis=0, tiled=True)  87 us
    all_gather x1, waiting for transfers between devices, per_device(): lax.all_gather(readout_matrix, 'dp', axis=0, tiled=True)  80.8 us
    reduce_scatter x1, waiting for transfers between devices, per_device(): lax.psum_scatter(contract_rows(normed, latent_grads), 'dp', scatter_dimen...  77.1 us
    all_to_all x1, blocking collectives, per_device(): lax.all_to_all(cotangents, 'dp', split_axis=1, concat_axis=0, tiled=True)  43.8 us
    dot_general x16, matrix products, multiply_trailing_factor(): lax.dot_general(left, right, (((1,), (1,)), ((), ())), preferred_element_...  24.7 us
  transfers between devices with their start and end apart: 44, of which 43 were waited for; matrix products, arithmetic and copies ran while one was open for 7% of the time, Pallas kernels for 0%

commit v1 on v0

--- a/solution.py
+++ b/solution.py
@@ -49,7 +49,9 @@
     down_full, up_full, entire_readout_matrix = (
         lax.all_gather(down_proj[0], "dp", axis=0, tiled=True),
         lax.all_gather(up_proj[0], "dp", axis=1, tiled=True),
-        lax.all_gather(readout_matrix, "dp", axis=0, tiled=True),
+        jnp.concatenate(
+            lax.all_to_all(jnp.stack([readout_matrix] * lax.axis_size("dp")), "dp", 0, 0), axis=0
+        ),
     )
     inputs = section_inputs[0]
     gain_row = norm_gain[0]

time: 935 us -> 851 us (0.910)
  waiting for transfers between devices: 714 us -> 623 us
    all_gather x1 -> x0, waiting for transfers between devices: 80.8 us -> none  [per_device(): lax.all_gather(readout_matrix, 'dp', axis=0, tiled=True)]
  transfers between devices with their start and end apart: 44 -> 44, of which waited for: 43 -> 42; matrix products, arithmetic and copies ran while one was open for 7% -> 8% of each run, Pallas kernels for 0% -> 0%
where the time goes in v1:
time: 851 us; the launch traced here: 849 us
  waiting for transfers between devices  623 us (73%)
  starting transfers between devices  94.6 us (11%)
  blocking collectives  43.9 us (5%)
  matrix products  32.6 us (4%)
  other arithmetic  31.5 us (4%)
  between operations  13.9 us (2%)
    ppermute x39, waiting for transfers between devices, from_behind(): return lax.ppermute(block, axis, route)  379 us
    ppermute x39, starting transfers between devices, from_behind(): return lax.ppermute(block, axis, route)  87 us
    all_gather x1, waiting for transfers between devices, per_device(): lax.all_gather(down_proj[0], 'dp', axis=0, tiled=True)  86.4 us
    all_gather x1, waiting for transfers between devices, per_device(): lax.all_gather(up_proj[0], 'dp', axis=1, tiled=True)  79.1 us
    reduce_scatter x1, waiting for transfers between devices, per_device(): lax.psum_scatter(contract_rows(normed, latent_grads), 'dp', scatter_dimen...  76.3 us
    all_to_all x1, blocking collectives, per_device(): lax.all_to_all(cotangents, 'dp', split_axis=1, concat_axis=0, tiled=True)  43.9 us
    dot_general x16, matrix products, multiply_trailing_factor(): lax.dot_general(left, right, (((1,), (1,)), ((), ())), preferred_element_...  24.7 us
  transfers between devices with their start and end apart: 44, of which 42 were waited for; matrix products, arithmetic and copies ran while one was open for 8% of the time, Pallas kernels for 0%

profile of v1, /device:TPU:448, one launch (start us, length us, event | category | flops | bytes accessed | tf_op | source)
XLA Modules:
  0.0 848.9 jit_solution(17135947919062615947)
XLA Ops:
  10.7 7.4 all-to-all-start
  18.6 86.4 %all-gather.8.cloned.1.call-done = bf16[1,4096,256]{2,1,0:T(8,128)(2,1)} async-done(((bf16[1,256,256]{2,1,0:T(8,128)(2,1)}), bf16[1,4096,256]{2,1,0:T(8,128)(2,1)}) %all-gather.8.cloned.1.call-update) | async-done | bytes 2097168 | tf_op jit(solution)/shard_map/all_gather | solution.py:50
  109.6 79.1 %all-gather.10.cloned.1.call-done = bf16[1,256,4096]{2,1,0:T(8,128)(2,1)} async-done(((bf16[1,256,256]{2,1,0:T(8,128)(2,1)}), bf16[1,256,4096]{2,1,0:T(8,128)(2,1)}) %all-gather.10.cloned.1.call-update) | async-done | bytes 2097168 | tf_op jit(solution)/shard_map/all_gather | solution.py:51
  192.2 521.3 %while.20 = (s32[]{:T(128)}, bf16[16,4096]{1,0:T(8,128)(2,1)S(1)}, bf16[8,16,4096]{2,1,0:T(8,128)(2,1)}, bf16[8,16,256]{2,1,0:T(8,128)(2,1)S(1)}, bf16[8,16,4096...) while((s32[]{:T(128)}, bf16[16,4096]{1,0:T(8,128)(2,1)S(1)}, ...), condition=%wide.region_7.8_spmd, body=%wide.region_3.7_spmd.sunk | while | flops 67805192 | bytes 15549357 | solution.py:138
  206.8 7.2 collective-permute-done
  216.0 10.5 %collective-permute-done = bf16[16,4096]{1,0:T(8,128)(2,1)S(1)} collective-permute-done((bf16[16,4096]{1,0:T(8,128)(2,1)S(1)}, bf16[16,4096]{1,0:T(8,128)(2,1)S(1)}, u32[]{:S(2)}, u32[]{:S(2)}) %collective-permute-start) | collective-permute-done | bytes 131104 | tf_op jit(solution)/shard_map/while/body/eval_jaxpr/ppermute | solution.py:12
  228.4 10.9 %collective-permute-done = bf16[16,4096]{1,0:T(8,128)(2,1)S(1)} collective-permute-done((bf16[16,4096]{1,0:T(8,128)(2,1)S(1)}, bf16[16,4096]{1,0:T(8,128)(2,1)S(1)}, u32[]{:S(2)}, u32[]{:S(2)}) %collective-permute-start) | collective-permute-done | bytes 131104 | tf_op jit(solution)/shard_map/while/body/eval_jaxpr/ppermute | solution.py:12
  241.3 11.0 %collective-permute-done = bf16[16,4096]{1,0:T(8,128)(2,1)S(1)} collective-permute-done((bf16[16,4096]{1,0:T(8,128)(2,1)S(1)}, bf16[16,4096]{1,0:T(8,128)(2,1)S(1)}, u32[]{:S(2)}, u32[]{:S(2)}) %collective-permute-start) | collective-permute-done | bytes 131104 | tf_op jit(solution)/shard_map/while/body/eval_jaxpr/ppermute | solution.py:12
  254.3 11.1 %collective-permute-done = bf16[16,4096]{1,0:T(8,128)(2,1)S(1)} collective-permute-done((bf16[16,4096]{1,0:T(8,128)(2,1)S(1)}, bf16[16,4096]{1,0:T(8,128)(2,1)S(1)}, u32[]{:S(2)}, u32[]{:S(2)}) %collective-permute-start) | collective-permute-done | bytes 131104 | tf_op jit(solution)/shard_map/while/body/eval_jaxpr/ppermute | solution.py:12
  267.4 10.7 %collective-permute-done = bf16[16,4096]{1,0:T(8,128)(2,1)S(1)} collective-permute-done((bf16[16,4096]{1,0:T(8,128)(2,1)S(1)}, bf16[16,4096]{1,0:T(8,128)(2,1)S(1)}, u32[]{:S(2)}, u32[]{:S(2)}) %collective-permute-start) | collective-permute-done | bytes 131104 | tf_op jit(solution)/shard_map/while/body/eval_jaxpr/ppermute | solution.py:12
  280.1 10.4 %collective-permute-done = bf16[16,4096]{1,0:T(8,128)(2,1)S(1)} collective-permute-done((bf16[16,4096]{1,0:T(8,128)(2,1)S(1)}, bf16[16,4096]{1,0:T(8,128)(2,1)S(1)}, u32[]{:S(2)}, u32[]{:S(2)}) %collective-permute-start) | collective-permute-done | bytes 131104 | tf_op jit(solution)/shard_map/while/body/eval_jaxpr/ppermute | solution.py:12
  292.5 10.4 %collective-permute-done = bf16[16,4096]{1,0:T(8,128)(2,1)S(1)} collective-permute-done((bf16[16,4096]{1,0:T(8,128)(2,1)S(1)}, bf16[16,4096]{1,0:T(8,128)(2,1)S(1)}, u32[]{:S(2)}, u32[]{:S(2)}) %collective-permute-start) | collective-permute-done | bytes 131104 | tf_op jit(solution)/shard_map/while/body/eval_jaxpr/ppermute | solution.py:12
  304.8 10.4 %collective-permute-done = bf16[16,4096]{1,0:T(8,128)(2,1)S(1)} collective-permute-done((bf16[16,4096]{1,0:T(8,128)(2,1)S(1)}, bf16[16,4096]{1,0:T(8,128)(2,1)S(1)}, u32[]{:S(2)}, u32[]{:S(2)}) %collective-permute-start) | collective-permute-done | bytes 131104 | tf_op jit(solution)/shard_map/while/body/eval_jaxpr/ppermute | solution.py:12
  317.1 10.4 %collective-permute-done = bf16[16,4096]{1,0:T(8,128)(2,1)S(1)} collective-permute-done((bf16[16,4096]{1,0:T(8,128)(2,1)S(1)}, bf16[16,4096]{1,0:T(8,128)(2,1)S(1)}, u32[]{:S(2)}, u32[]{:S(2)}) %collective-permute-start) | collective-permute-done | bytes 131104 | tf_op jit(solution)/shard_map/while/body/eval_jaxpr/ppermute | solution.py:12
  329.5 10.4 %collective-permute-done = bf16[16,4096]{1,0:T(8,128)(2,1)S(1)} collective-permute-done((bf16[16,4096]{1,0:T(8,128)(2,1)S(1)}, bf16[16,4096]{1,0:T(8,128)(2,1)S(1)}, u32[]{:S(2)}, u32[]{:S(2)}) %collective-permute-start) | collective-permute-done | bytes 131104 | tf_op jit(solution)/shard_map/while/body/eval_jaxpr/ppermute | solution.py:12
  341.8 10.4 %collective-permute-done = bf16[16,4096]{1,0:T(8,128)(2,1)S(1)} collective-permute-done((bf16[16,4096]{1,0:T(8,128)(2,1)S(1)}, bf16[16,4096]{1,0:T(8,128)(2,1)S(1)}, u32[]{:S(2)}, u32[]{:S(2)}) %collective-permute-start) | collective-permute-done | bytes 131104 | tf_op jit(solution)/shard_map/while/body/eval_jaxpr/ppermute | solution.py:12
  354.1 10.4 %collective-permute-done = bf16[16,4096]{1,0:T(8,128)(2,1)S(1)} collective-permute-done((bf16[16,4096]{1,0:T(8,128)(2,1)S(1)}, bf16[16,4096]{1,0:T(8,128)(2,1)S(1)}, u32[]{:S(2)}, u32[]{:S(2)}) %collective-permute-start) | collective-permute-done | bytes 131104 | tf_op jit(solution)/shard_map/while/body/eval_jaxpr/ppermute | solution.py:12
  366.5 10.4 %collective-permute-done = bf16[16,4096]{1,0:T(8,128)(2,1)S(1)} collective-permute-done((bf16[16,4096]{1,0:T(8,128)(2,1)S(1)}, bf16[16,4096]{1,0:T(8,128)(2,1)S(1)}, u32[]{:S(2)}, u32[]{:S(2)}) %collective-permute-start) | collective-permute-done | bytes 131104 | tf_op jit(solution)/shard_map/while/body/eval_jaxpr/ppermute | solution.py:12
  378.8 10.4 %collective-permute-done = bf16[16,4096]{1,0:T(8,128)(2,1)S(1)} collective-permute-done((bf16[16,4096]{1,0:T(8,128)(2,1)S(1)}, bf16[16,4096]{1,0:T(8,128)(2,1)S(1)}, u32[]{:S(2)}, u32[]{:S(2)}) %collective-permute-start) | collective-permute-done | bytes 131104 | tf_op jit(solution)/shard_map/while/body/eval_jaxpr/ppermute | solution.py:12
  391.1 17.0 %collective-permute-done = bf16[16,4096]{1,0:T(8,128)(2,1)S(1)} collective-permute-done((bf16[16,4096]{1,0:T(8,128)(2,1)S(1)}, bf16[16,4096]{1,0:T(8,128)(2,1)S(1)}, u32[]{:S(2)}, u32[]{:S(2)}) %collective-permute-start) | collective-permute-done | bytes 131104 | tf_op jit(solution)/shard_map/while/body/eval_jaxpr/ppermute | solution.py:12
  416.7 10.4 %collective-permute-done = bf16[16,4096]{1,0:T(8,128)(2,1)S(1)} collective-permute-done((bf16[16,4096]{1,0:T(8,128)(2,1)S(1)}, bf16[16,4096]{1,0:T(8,128)(2,1)S(1)}, u32[]{:S(2)}, u32[]{:S(2)}) %collective-permute-start) | collective-permute-done | bytes 131104 | tf_op jit(solution)/shard_map/while/body/eval_jaxpr/ppermute | solution.py:12
  435.6 10.4 %collective-permute-done = bf16[16,4096]{1,0:T(8,128)(2,1)S(1)} collective-permute-done((bf16[16,4096]{1,0:T(8,128)(2,1)S(1)}, bf16[16,4096]{1,0:T(8,128)(2,1)S(1)}, u32[]{:S(2)}, u32[]{:S(2)}) %collective-permute-start) | collective-permute-done | bytes 131104 | tf_op jit(solution)/shard_map/while/body/eval_jaxpr/ppermute | solution.py:12
  446.0 6.6 conditional.4
  454.6 10.3 %collective-permute-done = bf16[16,4096]{1,0:T(8,128)(2,1)S(1)} collective-permute-done((bf16[16,4096]{1,0:T(8,128)(2,1)S(1)}, bf16[16,4096]{1,0:T(8,128)(2,1)S(1)}, u32[]{:S(2)}, u32[]{:S(2)}) %collective-permute-start) | collective-permute-done | bytes 131104 | tf_op jit(solution)/shard_map/while/body/eval_jaxpr/ppermute | solution.py:12
  465.0 6.6 conditional.4
  473.5 10.4 %collective-permute-done = bf16[16,4096]{1,0:T(8,128)(2,1)S(1)} collective-permute-done((bf16[16,4096]{1,0:T(8,128)(2,1)S(1)}, bf16[16,4096]{1,0:T(8,128)(2,1)S(1)}, u32[]{:S(2)}, u32[]{:S(2)}) %collective-permute-start) | collective-permute-done | bytes 131104 | tf_op jit(solution)/shard_map/while/body/eval_jaxpr/ppermute | solution.py:12
  483.9 6.6 conditional.4
  492.5 10.4 %collective-permute-done = bf16[16,4096]{1,0:T(8,128)(2,1)S(1)} collective-permute-done((bf16[16,4096]{1,0:T(8,128)(2,1)S(1)}, bf16[16,4096]{1,0:T(8,128)(2,1)S(1)}, u32[]{:S(2)}, u32[]{:S(2)}) %collective-permute-start) | collective-permute-done | bytes 131104 | tf_op jit(solution)/shard_map/while/body/eval_jaxpr/ppermute | solution.py:12
  502.9 6.6 conditional.4
  511.5 10.3 %collective-permute-done = bf16[16,4096]{1,0:T(8,128)(2,1)S(1)} collective-permute-done((bf16[16,4096]{1,0:T(8,128)(2,1)S(1)}, bf16[16,4096]{1,0:T(8,128)(2,1)S(1)}, u32[]{:S(2)}, u32[]{:S(2)}) %collective-permute-start) | collective-permute-done | bytes 131104 | tf_op jit(solution)/shard_map/while/body/eval_jaxpr/ppermute | solution.py:12
  521.9 6.6 conditional.4
  530.4 10.4 %collective-permute-done = bf16[16,4096]{1,0:T(8,128)(2,1)S(1)} collective-permute-done((bf16[16,4096]{1,0:T(8,128)(2,1)S(1)}, bf16[16,4096]{1,0:T(8,128)(2,1)S(1)}, u32[]{:S(2)}, u32[]{:S(2)}) %collective-permute-start) | collective-permute-done | bytes 131104 | tf_op jit(solution)/shard_map/while/body/eval_jaxpr/ppermute | solution.py:12
  540.8 6.6 conditional.4
  553.2 9.1 %collective-permute-start = (bf16[16,4096]{1,0:T(8,128)(2,1)S(1)}, bf16[16,4096]{1,0:T(8,128)(2,1)S(1)}, u32[]{:S(2)}, u32[]{:S(2)}) collective-permute-start(bf16[16,4096]{1,0:T(8,128)(2,1)S(1)} %get-tuple-element.612), channel_id=1, source_target_pairs={{16,0},{32,16},{48,32},{64,48},{80,64},{96,80},{112,96},{128,112},... | collective-permute-start | bytes 393224 | tf_op jit(solution)/shard_map/while/body/eval_jaxpr/ppermute | solution.py:12
  568.6 9.2 %collective-permute-done = bf16[16,4096]{1,0:T(8,128)(2,1)S(1)} collective-permute-done((bf16[16,4096]{1,0:T(8,128)(2,1)S(1)}, bf16[16,4096]{1,0:T(8,128)(2,1)S(1)}, u32[]{:S(2)}, u32[]{:S(2)}) %collective-permute-start) | collective-permute-done | bytes 131104 | tf_op jit(solution)/shard_map/while/body/eval_jaxpr/ppermute | solution.py:12
  579.8 10.4 %collective-permute-done = bf16[16,4096]{1,0:T(8,128)(2,1)S(1)} collective-permute-done((bf16[16,4096]{1,0:T(8,128)(2,1)S(1)}, bf16[16,4096]{1,0:T(8,128)(2,1)S(1)}, u32[]{:S(2)}, u32[]{:S(2)}) %collective-permute-start) | collective-permute-done | bytes 131104 | tf_op jit(solution)/shard_map/while/body/eval_jaxpr/ppermute | solution.py:12
  592.1 10.4 %collective-permute-done = bf16[16,4096]{1,0:T(8,128)(2,1)S(1)} collective-permute-done((bf16[16,4096]{1,0:T(8,128)(2,1)S(1)}, bf16[16,4096]{1,0:T(8,128)(2,1)S(1)}, u32[]{:S(2)}, u32[]{:S(2)}) %collective-permute-start) | collective-permute-done | bytes 131104 | tf_op jit(solution)/shard_map/while/body/eval_jaxpr/ppermute | solution.py:12
  604.5 10.4 %collective-permute-done = bf16[16,4096]{1,0:T(8,128)(2,1)S(1)} collective-permute-done((bf16[16,4096]{1,0:T(8,128)(2,1)S(1)}, bf16[16,4096]{1,0:T(8,128)(2,1)S(1)}, u32[]{:S(2)}, u32[]{:S(2)}) %collective-permute-start) | collective-permute-done | bytes 131104 | tf_op jit(solution)/shard_map/while/body/eval_jaxpr/ppermute | solution.py:12
  616.8 10.4 %collective-permute-done = bf16[16,4096]{1,0:T(8,128)(2,1)S(1)} collective-permute-done((bf16[16,4096]{1,0:T(8,128)(2,1)S(1)}, bf16[16,4096]{1,0:T(8,128)(2,1)S(1)}, u32[]{:S(2)}, u32[]{:S(2)}) %collective-permute-start) | collective-permute-done | bytes 131104 | tf_op jit(solution)/shard_map/while/body/eval_jaxpr/ppermute | solution.py:12
  629.1 10.4 %collective-permute-done = bf16[16,4096]{1,0:T(8,128)(2,1)S(1)} collective-permute-done((bf16[16,4096]{1,0:T(8,128)(2,1)S(1)}, bf16[16,4096]{1,0:T(8,128)(2,1)S(1)}, u32[]{:S(2)}, u32[]{:S(2)}) %collective-permute-start) | collective-permute-done | bytes 131104 | tf_op jit(solution)/shard_map/while/body/eval_jaxpr/ppermute | solution.py:12
  641.5 10.4 %collective-permute-done = bf16[16,4096]{1,0:T(8,128)(2,1)S(1)} collective-permute-done((bf16[16,4096]{1,0:T(8,128)(2,1)S(1)}, bf16[16,4096]{1,0:T(8,128)(2,1)S(1)}, u32[]{:S(2)}, u32[]{:S(2)}) %collective-permute-start) | collective-permute-done | bytes 131104 | tf_op jit(solution)/shard_map/while/body/eval_jaxpr/ppermute | solution.py:12
  653.8 10.4 %collective-permute-done = bf16[16,4096]{1,0:T(8,128)(2,1)S(1)} collective-permute-done((bf16[16,4096]{1,0:T(8,128)(2,1)S(1)}, bf16[16,4096]{1,0:T(8,128)(2,1)S(1)}, u32[]{:S(2)}, u32[]{:S(2)}) %collective-permute-start) | collective-permute-done | bytes 131104 | tf_op jit(solution)/shard_map/while/body/eval_jaxpr/ppermute | solution.py:12
  666.1 10.4 %collective-permute-done = bf16[16,4096]{1,0:T(8,128)(2,1)S(1)} collective-permute-done((bf16[16,4096]{1,0:T(8,128)(2,1)S(1)}, bf16[16,4096]{1,0:T(8,128)(2,1)S(1)}, u32[]{:S(2)}, u32[]{:S(2)}) %collective-permute-start) | collective-permute-done | bytes 131104 | tf_op jit(solution)/shard_map/while/body/eval_jaxpr/ppermute | solution.py:12
  678.5 10.4 %collective-permute-done = bf16[16,4096]{1,0:T(8,128)(2,1)S(1)} collective-permute-done((bf16[16,4096]{1,0:T(8,128)(2,1)S(1)}, bf16[16,4096]{1,0:T(8,128)(2,1)S(1)}, u32[]{:S(2)}, u32[]{:S(2)}) %collective-permute-start) | collective-permute-done | bytes 131104 | tf_op jit(solution)/shard_map/while/body/eval_jaxpr/ppermute | solution.py:12
  690.8 10.4 %collective-permute-done = bf16[16,4096]{1,0:T(8,128)(2,1)S(1)} collective-permute-done((bf16[16,4096]{1,0:T(8,128)(2,1)S(1)}, bf16[16,4096]{1,0:T(8,128)(2,1)S(1)}, u32[]{:S(2)}, u32[]{:S(2)}) %collective-permute-start) | collective-permute-done | bytes 131104 | tf_op jit(solution)/shard_map/while/body/eval_jaxpr/ppermute | solution.py:12
  703.1 10.4 %collective-permute-done = bf16[16,4096]{1,0:T(8,128)(2,1)S(1)} collective-permute-done((bf16[16,4096]{1,0:T(8,128)(2,1)S(1)}, bf16[16,4096]{1,0:T(8,128)(2,1)S(1)}, u32[]{:S(2)}, u32[]{:S(2)}) %collective-permute-start) | collective-permute-done | bytes 131104 | tf_op jit(solution)/shard_map/while/body/eval_jaxpr/ppermute | solution.py:12
  718.1 43.9 %all_to_all.24 = bf16[128,16,256]{2,0,1:T(8,128)(2,1)S(1)} all-to-all(bf16[128,16,256]{2,0,1:T(8,128)(2,1)S(1)} %copy.16), channel_id=1, replica_groups=mesh['section'=32,'dp'=16] {'dp'}, dimensions={1} | all-to-all | bytes 2097152 | tf_op jit(solution)/shard_map/all_to_all | solution.py:146
  764.4 76.3 %reduce-scatter.2.cloned.1.call-done = f32[256,256]{1,0:T(8,128)} async-done(((f32[4096,256]{1,0:T(8,128)}), f32[256,256]{1,0:T(8,128)}) %reduce-scatter.2.cloned.1.call-update) | async-done | bytes 262160 | tf_op jit(solution)/shard_map/reduce_scatter | solution.py:142
  (231 shorter events, 177.7 us)
Async XLA Ops:
  7.2 11.1 %copy-start.2 = (bf16[1,128,4096]{2,1,0:T(8,128)(2,1)S(1)}, bf16[1,128,4096]{2,1,0:T(8,128)(2,1)}, u32[]{:S(2)}) copy-start(bf16[1,128,4096]{2,1,0:T(8,128)(2,1)} %param.13) | copy-start | bytes 3145732
  7.2 97.8 %all-gather.8.cloned.1.call-start = ((), (), s32[]{:S(2)}) async-start(), calls=%async_computation.5 | async-start | bytes 2228224 | tf_op jit(solution)/shard_map/all_gather | solution.py:50
  7.9 180.8 %all-gather.10.cloned.1.call-start = ((), (), s32[]{:S(2)}) async-start(), calls=%async_computation.6 | async-start | bytes 2228224 | tf_op jit(solution)/shard_map/all_gather | solution.py:51
  10.7 99.0 %all-to-all-start = ((bf16[16,256,128]{2,1,0:T(8,128)(2,1)}), bf16[16,256,128]{2,1,0:T(8,128)(2,1)S(1)}, u32[]{:S(2)}, u32[]{:S(2)}) async-start(bf16[16,256,128]{2,1,0:T(8,128)(2,1)} %stack.2), calls=%async_computation | async-start | bytes 2097152 | tf_op jit(solution)/shard_map/all_to_all | solution.py:53
  18.1 743.9 %all-gather.6.cloned.1.call-start = ((), (), s32[]{:S(2)}) async-start(), calls=%async_computation.4 | async-start | bytes 1114112 | tf_op jit(solution)/shard_map/all_gather | solution.py:145
  18.6 89.4 %copy-start.7 = (s32[8]{0:T(128)S(1)}, s32[8]{0:T(128)}, u32[]{:S(2)}) copy-start(s32[8]{0:T(128)} %param.19) | copy-start | bytes 100
  107.8 81.0 %copy-start.4 = (bf16[128,256]{1,0:T(8,128)(2,1)S(1)}, bf16[128,256]{1,0:T(8,128)(2,1)}, u32[]{:S(2)}) copy-start(bf16[128,256]{1,0:T(8,128)(2,1)} %get-tuple-element.491) | copy-start | bytes 196612
  107.8 81.0 %copy-start.5 = (f32[128,128]{1,0:T(8,128)S(1)}, f32[128,128]{1,0:T(8,128)}, u32[]{:S(2)}) copy-start(f32[128,128]{1,0:T(8,128)} %param.18) | copy-start | bytes 196612
  107.8 732.9 %reduce-scatter.2.cloned.1.call-start = ((), (), s32[]{:S(2)}) async-start(), calls=%async_computation.3 | async-start | bytes 4456448 | tf_op jit(solution)/shard_map/reduce_scatter | solution.py:142
  192.2 4.4 collective-permute-start
  196.7 6.3 collective-permute-start
  203.0 11.0 %collective-permute-start = (bf16[16,4096]{1,0:T(8,128)(2,1)S(1)}, bf16[16,4096]{1,0:T(8,128)(2,1)S(1)}, u32[]{:S(2)}, u32[]{:S(2)}) collective-permute-start(bf16[16,4096]{1,0:T(8,128)(2,1)S(1)} %get-tuple-element.612), channel_id=1, source_target_pairs={{16,0},{32,16},{48,32},{64,48},{80,64},{96,80},{112,96},{128,112},... | collective-permute-start | bytes 393224 | tf_op jit(solution)/shard_map/while/body/eval_jaxpr/ppermute | solution.py:12
  214.0 12.4 %collective-permute-start = (bf16[16,4096]{1,0:T(8,128)(2,1)S(1)}, bf16[16,4096]{1,0:T(8,128)(2,1)S(1)}, u32[]{:S(2)}, u32[]{:S(2)}) collective-permute-start(bf16[16,4096]{1,0:T(8,128)(2,1)S(1)} %get-tuple-element.612), channel_id=1, source_target_pairs={{16,0},{32,16},{48,32},{64,48},{80,64},{96,80},{112,96},{128,112},... | collective-permute-start | bytes 393224 | tf_op jit(solution)/shard_map/while/body/eval_jaxpr/ppermute | solution.py:12
  226.5 12.9 %collective-permute-start = (bf16[16,4096]{1,0:T(8,128)(2,1)S(1)}, bf16[16,4096]{1,0:T(8,128)(2,1)S(1)}, u32[]{:S(2)}, u32[]{:S(2)}) collective-permute-start(bf16[16,4096]{1,0:T(8,128)(2,1)S(1)} %get-tuple-element.612), channel_id=1, source_target_pairs={{16,0},{32,16},{48,32},{64,48},{80,64},{96,80},{112,96},{128,112},... | collective-permute-start | bytes 393224 | tf_op jit(solution)/shard_map/while/body/eval_jaxpr/ppermute | solution.py:12
  239.4 13.0 %collective-permute-start = (bf16[16,4096]{1,0:T(8,128)(2,1)S(1)}, bf16[16,4096]{1,0:T(8,128)(2,1)S(1)}, u32[]{:S(2)}, u32[]{:S(2)}) collective-permute-start(bf16[16,4096]{1,0:T(8,128)(2,1)S(1)} %get-tuple-element.612), channel_id=1, source_target_pairs={{16,0},{32,16},{48,32},{64,48},{80,64},{96,80},{112,96},{128,112},... | collective-permute-start | bytes 393224 | tf_op jit(solution)/shard_map/while/body/eval_jaxpr/ppermute | solution.py:12
  252.4 13.1 %collective-permute-start = (bf16[16,4096]{1,0:T(8,128)(2,1)S(1)}, bf16[16,4096]{1,0:T(8,128)(2,1)S(1)}, u32[]{:S(2)}, u32[]{:S(2)}) collective-permute-start(bf16[16,4096]{1,0:T(8,128)(2,1)S(1)} %get-tuple-element.612), channel_id=1, source_target_pairs={{16,0},{32,16},{48,32},{64,48},{80,64},{96,80},{112,96},{128,112},... | collective-permute-start | bytes 393224 | tf_op jit(solution)/shard_map/while/body/eval_jaxpr/ppermute | solution.py:12
  265.5 12.7 %collective-permute-start = (bf16[16,4096]{1,0:T(8,128)(2,1)S(1)}, bf16[16,4096]{1,0:T(8,128)(2,1)S(1)}, u32[]{:S(2)}, u32[]{:S(2)}) collective-permute-start(bf16[16,4096]{1,0:T(8,128)(2,1)S(1)} %get-tuple-element.612), channel_id=1, source_target_pairs={{16,0},{32,16},{48,32},{64,48},{80,64},{96,80},{112,96},{128,112},... | collective-permute-start | bytes 393224 | tf_op jit(solution)/shard_map/while/body/eval_jaxpr/ppermute | solution.py:12
  278.2 12.3 %collective-permute-start = (bf16[16,4096]{1,0:T(8,128)(2,1)S(1)}, bf16[16,4096]{1,0:T(8,128)(2,1)S(1)}, u32[]{:S(2)}, u32[]{:S(2)}) collective-permute-start(bf16[16,4096]{1,0:T(8,128)(2,1)S(1)} %get-tuple-element.612), channel_id=1, source_target_pairs={{16,0},{32,16},{48,32},{64,48},{80,64},{96,80},{112,96},{128,112},... | collective-permute-start | bytes 393224 | tf_op jit(solution)/shard_map/while/body/eval_jaxpr/ppermute | solution.py:12
  290.5 12.3 %collective-permute-start = (bf16[16,4096]{1,0:T(8,128)(2,1)S(1)}, bf16[16,4096]{1,0:T(8,128)(2,1)S(1)}, u32[]{:S(2)}, u32[]{:S(2)}) collective-permute-start(bf16[16,4096]{1,0:T(8,128)(2,1)S(1)} %get-tuple-element.612), channel_id=1, source_target_pairs={{16,0},{32,16},{48,32},{64,48},{80,64},{96,80},{112,96},{128,112},... | collective-permute-start | bytes 393224 | tf_op jit(solution)/shard_map/while/body/eval_jaxpr/ppermute | solution.py:12
  302.9 12.3 %collective-permute-start = (bf16[16,4096]{1,0:T(8,128)(2,1)S(1)}, bf16[16,4096]{1,0:T(8,128)(2,1)S(1)}, u32[]{:S(2)}, u32[]{:S(2)}) collective-permute-start(bf16[16,4096]{1,0:T(8,128)(2,1)S(1)} %get-tuple-element.612), channel_id=1, source_target_pairs={{16,0},{32,16},{48,32},{64,48},{80,64},{96,80},{112,96},{128,112},... | collective-permute-start | bytes 393224 | tf_op jit(solution)/shard_map/while/body/eval_jaxpr/ppermute | solution.py:12
  315.2 12.3 %collective-permute-start = (bf16[16,4096]{1,0:T(8,128)(2,1)S(1)}, bf16[16,4096]{1,0:T(8,128)(2,1)S(1)}, u32[]{:S(2)}, u32[]{:S(2)}) collective-permute-start(bf16[16,4096]{1,0:T(8,128)(2,1)S(1)} %get-tuple-element.612), channel_id=1, source_target_pairs={{16,0},{32,16},{48,32},{64,48},{80,64},{96,80},{112,96},{128,112},... | collective-permute-start | bytes 393224 | tf_op jit(solution)/shard_map/while/body/eval_jaxpr/ppermute | solution.py:12
  327.5 12.3 %collective-permute-start = (bf16[16,4096]{1,0:T(8,128)(2,1)S(1)}, bf16[16,4096]{1,0:T(8,128)(2,1)S(1)}, u32[]{:S(2)}, u32[]{:S(2)}) collective-permute-start(bf16[16,4096]{1,0:T(8,128)(2,1)S(1)} %get-tuple-element.612), channel_id=1, source_target_pairs={{16,0},{32,16},{48,32},{64,48},{80,64},{96,80},{112,96},{128,112},... | collective-permute-start | bytes 393224 | tf_op jit(solution)/shard_map/while/body/eval_jaxpr/ppermute | solution.py:12
  339.9 12.3 %collective-permute-start = (bf16[16,4096]{1,0:T(8,128)(2,1)S(1)}, bf16[16,4096]{1,0:T(8,128)(2,1)S(1)}, u32[]{:S(2)}, u32[]{:S(2)}) collective-permute-start(bf16[16,4096]{1,0:T(8,128)(2,1)S(1)} %get-tuple-element.612), channel_id=1, source_target_pairs={{16,0},{32,16},{48,32},{64,48},{80,64},{96,80},{112,96},{128,112},... | collective-permute-start | bytes 393224 | tf_op jit(solution)/shard_map/while/body/eval_jaxpr/ppermute | solution.py:12
  352.2 12.3 %collective-permute-start = (bf16[16,4096]{1,0:T(8,128)(2,1)S(1)}, bf16[16,4096]{1,0:T(8,128)(2,1)S(1)}, u32[]{:S(2)}, u32[]{:S(2)}) collective-permute-start(bf16[16,4096]{1,0:T(8,128)(2,1)S(1)} %get-tuple-element.612), channel_id=1, source_target_pairs={{16,0},{32,16},{48,32},{64,48},{80,64},{96,80},{112,96},{128,112},... | collective-permute-start | bytes 393224 | tf_op jit(solution)/shard_map/while/body/eval_jaxpr/ppermute | solution.py:12
  364.5 12.3 %collective-permute-start = (bf16[16,4096]{1,0:T(8,128)(2,1)S(1)}, bf16[16,4096]{1,0:T(8,128)(2,1)S(1)}, u32[]{:S(2)}, u32[]{:S(2)}) collective-permute-start(bf16[16,4096]{1,0:T(8,128)(2,1)S(1)} %get-tuple-element.612), channel_id=1, source_target_pairs={{16,0},{32,16},{48,32},{64,48},{80,64},{96,80},{112,96},{128,112},... | collective-permute-start | bytes 393224 | tf_op jit(solution)/shard_map/while/body/eval_jaxpr/ppermute | solution.py:12
  376.9 12.3 %collective-permute-start = (bf16[16,4096]{1,0:T(8,128)(2,1)S(1)}, bf16[16,4096]{1,0:T(8,128)(2,1)S(1)}, u32[]{:S(2)}, u32[]{:S(2)}) collective-permute-start(bf16[16,4096]{1,0:T(8,128)(2,1)S(1)} %get-tuple-element.612), channel_id=1, source_target_pairs={{16,0},{32,16},{48,32},{64,48},{80,64},{96,80},{112,96},{128,112},... | collective-permute-start | bytes 393224 | tf_op jit(solution)/shard_map/while/body/eval_jaxpr/ppermute | solution.py:12
  389.2 18.9 %collective-permute-start = (bf16[16,4096]{1,0:T(8,128)(2,1)S(1)}, bf16[16,4096]{1,0:T(8,128)(2,1)S(1)}, u32[]{:S(2)}, u32[]{:S(2)}) collective-permute-start(bf16[16,4096]{1,0:T(8,128)(2,1)S(1)} %get-tuple-element.612), channel_id=1, source_target_pairs={{16,0},{32,16},{48,32},{64,48},{80,64},{96,80},{112,96},{128,112},... | collective-permute-start | bytes 393224 | tf_op jit(solution)/shard_map/while/body/eval_jaxpr/ppermute | solution.py:12
  414.8 12.3 %collective-permute-start = (bf16[16,4096]{1,0:T(8,128)(2,1)S(1)}, bf16[16,4096]{1,0:T(8,128)(2,1)S(1)}, u32[]{:S(2)}, u32[]{:S(2)}) collective-permute-start(bf16[16,4096]{1,0:T(8,128)(2,1)S(1)} %get-tuple-element.612), channel_id=1, source_target_pairs={{16,0},{32,16},{48,32},{64,48},{80,64},{96,80},{112,96},{128,112},... | collective-permute-start | bytes 393224 | tf_op jit(solution)/shard_map/while/body/eval_jaxpr/ppermute | solution.py:12
  433.7 12.3 %collective-permute-start = (bf16[16,4096]{1,0:T(8,128)(2,1)S(1)}, bf16[16,4096]{1,0:T(8,128)(2,1)S(1)}, u32[]{:S(2)}, u32[]{:S(2)}) collective-permute-start(bf16[16,4096]{1,0:T(8,128)(2,1)S(1)} %get-tuple-element.612), channel_id=1, source_target_pairs={{16,0},{32,16},{48,32},{64,48},{80,64},{96,80},{112,96},{128,112},... | collective-permute-start | bytes 393224 | tf_op jit(solution)/shard_map/while/body/eval_jaxpr/ppermute | solution.py:12
  452.7 12.3 %collective-permute-start = (bf16[16,4096]{1,0:T(8,128)(2,1)S(1)}, bf16[16,4096]{1,0:T(8,128)(2,1)S(1)}, u32[]{:S(2)}, u32[]{:S(2)}) collective-permute-start(bf16[16,4096]{1,0:T(8,128)(2,1)S(1)} %get-tuple-element.612), channel_id=1, source_target_pairs={{16,0},{32,16},{48,32},{64,48},{80,64},{96,80},{112,96},{128,112},... | collective-permute-start | bytes 393224 | tf_op jit(solution)/shard_map/while/body/eval_jaxpr/ppermute | solution.py:12
  471.6 12.3 %collective-permute-start = (bf16[16,4096]{1,0:T(8,128)(2,1)S(1)}, bf16[16,4096]{1,0:T(8,128)(2,1)S(1)}, u32[]{:S(2)}, u32[]{:S(2)}) collective-permute-start(bf16[16,4096]{1,0:T(8,128)(2,1)S(1)} %get-tuple-element.612), channel_id=1, source_target_pairs={{16,0},{32,16},{48,32},{64,48},{80,64},{96,80},{112,96},{128,112},... | collective-permute-start | bytes 393224 | tf_op jit(solution)/shard_map/while/body/eval_jaxpr/ppermute | solution.py:12
  490.6 12.3 %collective-permute-start = (bf16[16,4096]{1,0:T(8,128)(2,1)S(1)}, bf16[16,4096]{1,0:T(8,128)(2,1)S(1)}, u32[]{:S(2)}, u32[]{:S(2)}) collective-permute-start(bf16[16,4096]{1,0:T(8,128)(2,1)S(1)} %get-tuple-element.612), channel_id=1, source_target_pairs={{16,0},{32,16},{48,32},{64,48},{80,64},{96,80},{112,96},{128,112},... | collective-permute-start | bytes 393224 | tf_op jit(solution)/shard_map/while/body/eval_jaxpr/ppermute | solution.py:12
  509.6 12.3 %collective-permute-start = (bf16[16,4096]{1,0:T(8,128)(2,1)S(1)}, bf16[16,4096]{1,0:T(8,128)(2,1)S(1)}, u32[]{:S(2)}, u32[]{:S(2)}) collective-permute-start(bf16[16,4096]{1,0:T(8,128)(2,1)S(1)} %get-tuple-element.612), channel_id=1, source_target_pairs={{16,0},{32,16},{48,32},{64,48},{80,64},{96,80},{112,96},{128,112},... | collective-permute-start | bytes 393224 | tf_op jit(solution)/shard_map/while/body/eval_jaxpr/ppermute | solution.py:12
  528.5 12.3 %collective-permute-start = (bf16[16,4096]{1,0:T(8,128)(2,1)S(1)}, bf16[16,4096]{1,0:T(8,128)(2,1)S(1)}, u32[]{:S(2)}, u32[]{:S(2)}) collective-permute-start(bf16[16,4096]{1,0:T(8,128)(2,1)S(1)} %get-tuple-element.612), channel_id=1, source_target_pairs={{16,0},{32,16},{48,32},{64,48},{80,64},{96,80},{112,96},{128,112},... | collective-permute-start | bytes 393224 | tf_op jit(solution)/shard_map/while/body/eval_jaxpr/ppermute | solution.py:12
  547.5 5.7 collective-permute-start
  553.2 12.3 %collective-permute-start = (bf16[16,4096]{1,0:T(8,128)(2,1)S(1)}, bf16[16,4096]{1,0:T(8,128)(2,1)S(1)}, u32[]{:S(2)}, u32[]{:S(2)}) collective-permute-start(bf16[16,4096]{1,0:T(8,128)(2,1)S(1)} %get-tuple-element.612), channel_id=1, source_target_pairs={{16,0},{32,16},{48,32},{64,48},{80,64},{96,80},{112,96},{128,112},... | collective-permute-start | bytes 393224 | tf_op jit(solution)/shard_map/while/body/eval_jaxpr/ppermute | solution.py:12
  565.5 12.3 %collective-permute-start = (bf16[16,4096]{1,0:T(8,128)(2,1)S(1)}, bf16[16,4096]{1,0:T(8,128)(2,1)S(1)}, u32[]{:S(2)}, u32[]{:S(2)}) collective-permute-start(bf16[16,4096]{1,0:T(8,128)(2,1)S(1)} %get-tuple-element.612), channel_id=1, source_target_pairs={{16,0},{32,16},{48,32},{64,48},{80,64},{96,80},{112,96},{128,112},... | collective-permute-start | bytes 393224 | tf_op jit(solution)/shard_map/while/body/eval_jaxpr/ppermute | solution.py:12
  577.8 12.3 %collective-permute-start = (bf16[16,4096]{1,0:T(8,128)(2,1)S(1)}, bf16[16,4096]{1,0:T(8,128)(2,1)S(1)}, u32[]{:S(2)}, u32[]{:S(2)}) collective-permute-start(bf16[16,4096]{1,0:T(8,128)(2,1)S(1)} %get-tuple-element.612), channel_id=1, source_target_pairs={{16,0},{32,16},{48,32},{64,48},{80,64},{96,80},{112,96},{128,112},... | collective-permute-start | bytes 393224 | tf_op jit(solution)/shard_map/while/body/eval_jaxpr/ppermute | solution.py:12
  590.2 12.3 %collective-permute-start = (bf16[16,4096]{1,0:T(8,128)(2,1)S(1)}, bf16[16,4096]{1,0:T(8,128)(2,1)S(1)}, u32[]{:S(2)}, u32[]{:S(2)}) collective-permute-start(bf16[16,4096]{1,0:T(8,128)(2,1)S(1)} %get-tuple-element.612), channel_id=1, source_target_pairs={{16,0},{32,16},{48,32},{64,48},{80,64},{96,80},{112,96},{128,112},... | collective-permute-start | bytes 393224 | tf_op jit(solution)/shard_map/while/body/eval_jaxpr/ppermute | solution.py:12
  602.5 12.3 %collective-permute-start = (bf16[16,4096]{1,0:T(8,128)(2,1)S(1)}, bf16[16,4096]{1,0:T(8,128)(2,1)S(1)}, u32[]{:S(2)}, u32[]{:S(2)}) collective-permute-start(bf16[16,4096]{1,0:T(8,128)(2,1)S(1)} %get-tuple-element.612), channel_id=1, source_target_pairs={{16,0},{32,16},{48,32},{64,48},{80,64},{96,80},{112,96},{128,112},... | collective-permute-start | bytes 393224 | tf_op jit(solution)/shard_map/while/body/eval_jaxpr/ppermute | solution.py:12
  614.8 12.3 %collective-permute-start = (bf16[16,4096]{1,0:T(8,128)(2,1)S(1)}, bf16[16,4096]{1,0:T(8,128)(2,1)S(1)}, u32[]{:S(2)}, u32[]{:S(2)}) collective-permute-start(bf16[16,4096]{1,0:T(8,128)(2,1)S(1)} %get-tuple-element.612), channel_id=1, source_target_pairs={{16,0},{32,16},{48,32},{64,48},{80,64},{96,80},{112,96},{128,112},... | collective-permute-start | bytes 393224 | tf_op jit(solution)/shard_map/while/body/eval_jaxpr/ppermute | solution.py:12
  627.2 12.3 %collective-permute-start = (bf16[16,4096]{1,0:T(8,128)(2,1)S(1)}, bf16[16,4096]{1,0:T(8,128)(2,1)S(1)}, u32[]{:S(2)}, u32[]{:S(2)}) collective-permute-start(bf16[16,4096]{1,0:T(8,128)(2,1)S(1)} %get-tuple-element.612), channel_id=1, source_target_pairs={{16,0},{32,16},{48,32},{64,48},{80,64},{96,80},{112,96},{128,112},... | collective-permute-start | bytes 393224 | tf_op jit(solution)/shard_map/while/body/eval_jaxpr/ppermute | solution.py:12
  639.5 12.3 %collective-permute-start = (bf16[16,4096]{1,0:T(8,128)(2,1)S(1)}, bf16[16,4096]{1,0:T(8,128)(2,1)S(1)}, u32[]{:S(2)}, u32[]{:S(2)}) collective-permute-start(bf16[16,4096]{1,0:T(8,128)(2,1)S(1)} %get-tuple-element.612), channel_id=1, source_target_pairs={{16,0},{32,16},{48,32},{64,48},{80,64},{96,80},{112,96},{128,112},... | collective-permute-start | bytes 393224 | tf_op jit(solution)/shard_map/while/body/eval_jaxpr/ppermute | solution.py:12
  651.9 12.3 %collective-permute-start = (bf16[16,4096]{1,0:T(8,128)(2,1)S(1)}, bf16[16,4096]{1,0:T(8,128)(2,1)S(1)}, u32[]{:S(2)}, u32[]{:S(2)}) collective-permute-start(bf16[16,4096]{1,0:T(8,128)(2,1)S(1)} %get-tuple-element.612), channel_id=1, source_target_pairs={{16,0},{32,16},{48,32},{64,48},{80,64},{96,80},{112,96},{128,112},... | collective-permute-start | bytes 393224 | tf_op jit(solution)/shard_map/while/body/eval_jaxpr/ppermute | solution.py:12
  664.2 12.3 %collective-permute-start = (bf16[16,4096]{1,0:T(8,128)(2,1)S(1)}, bf16[16,4096]{1,0:T(8,128)(2,1)S(1)}, u32[]{:S(2)}, u32[]{:S(2)}) collective-permute-start(bf16[16,4096]{1,0:T(8,128)(2,1)S(1)} %get-tuple-element.612), channel_id=1, source_target_pairs={{16,0},{32,16},{48,32},{64,48},{80,64},{96,80},{112,96},{128,112},... | collective-permute-start | bytes 393224 | tf_op jit(solution)/shard_map/while/body/eval_jaxpr/ppermute | solution.py:12
  676.5 12.3 %collective-permute-start = (bf16[16,4096]{1,0:T(8,128)(2,1)S(1)}, bf16[16,4096]{1,0:T(8,128)(2,1)S(1)}, u32[]{:S(2)}, u32[]{:S(2)}) collective-permute-start(bf16[16,4096]{1,0:T(8,128)(2,1)S(1)} %get-tuple-element.612), channel_id=1, source_target_pairs={{16,0},{32,16},{48,32},{64,48},{80,64},{96,80},{112,96},{128,112},... | collective-permute-start | bytes 393224 | tf_op jit(solution)/shard_map/while/body/eval_jaxpr/ppermute | solution.py:12
  688.9 12.3 %collective-permute-start = (bf16[16,4096]{1,0:T(8,128)(2,1)S(1)}, bf16[16,4096]{1,0:T(8,128)(2,1)S(1)}, u32[]{:S(2)}, u32[]{:S(2)}) collective-permute-start(bf16[16,4096]{1,0:T(8,128)(2,1)S(1)} %get-tuple-element.612), channel_id=1, source_target_pairs={{16,0},{32,16},{48,32},{64,48},{80,64},{96,80},{112,96},{128,112},... | collective-permute-start | bytes 393224 | tf_op jit(solution)/shard_map/while/body/eval_jaxpr/ppermute | solution.py:12
  701.2 12.3 %collective-permute-start = (bf16[16,4096]{1,0:T(8,128)(2,1)S(1)}, bf16[16,4096]{1,0:T(8,128)(2,1)S(1)}, u32[]{:S(2)}, u32[]{:S(2)}) collective-permute-start(bf16[16,4096]{1,0:T(8,128)(2,1)S(1)} %get-tuple-element.612), channel_id=1, source_target_pairs={{16,0},{32,16},{48,32},{64,48},{80,64},{96,80},{112,96},{128,112},... | collective-permute-start | bytes 393224 | tf_op jit(solution)/shard_map/while/body/eval_jaxpr/ppermute | solution.py:12
  (11 other events, 39.5 us)
Sparse Core Ops, SparseCore 0:
  10.1 94.8 all-gather.7
  107.0 81.6 all-gather.9
  191.4 83.3 all-gather.5
  716.4 124.2 reduce-scatter.1
